TPU v7x, 32 devices: a whole 2x2x4 slice. The times are simulated.
32 devices in a mesh: band: 2 (over core), grid: 16 (over z, y, x).
Axes of the slice: x: 2, y: 2, z: 4, core: 2. Of those that a mesh axis runs over, the one named last changes fastest.
Arguments:
- coefficients: float32 [4, 2, 128, 128, 128], P('band', None, 'grid'), may hold values from -0.01171875 to 0.01171875
- potential: float32 [128, 128, 128], P('grid'), may hold values from -3 to 3
- external: float32 [128, 128, 128], P('grid'), may hold values from -6 to 6
- core_density: float32 [128, 128, 128], P('grid'), may hold values from 0.05 to 0.5
- rotations: float32 [2, 4, 2], P(None, 'band'), may hold values from -2 to 3
- mlp_in: float32 [3, 32], replicated, may hold values from -4 to 4
- mlp_out: float32 [32], replicated, may hold values from -0.4 to 0.4
Outputs:
- new_coefficients: float32 [4, 2, 128, 128, 128], P('band', None, 'grid')
- new_potential: float32 [128, 128, 128], P('grid')
All inputs are finite; a program needn't handle non-finite values.
Results may differ from a plain program's by a relative error of at most 0.0003.
Values sent between devices are 32-bit elements; how exact they have to be, the bound alone decides.
A program may use at most 64 MiB of HBM per device.

v0:
```python
import functools
import math

import jax
import jax.numpy as jnp
import numpy as np
from jax import lax
from jax.experimental import pallas as pl
from jax.experimental.pallas import tpu as pltpu
from jax.sharding import PartitionSpec as P

MESH = pl.DeviceIdType.MESH
F32 = jnp.float32
BF16 = jnp.bfloat16

step_size = 0.2
epsilon = 1e-06
spacing = 0.58
kinetic_scale = 0.5 * (2.0 * math.pi / spacing) ** 2
coulomb_scale = spacing * spacing / math.pi
gradient_scale = 2.0 * math.pi / spacing
reduced_scale = 2.0 * (3.0 * math.pi * math.pi) ** (1.0 / 3.0)
exchange_scale = (3.0 / math.pi) ** (1.0 / 3.0)


def halves(table):
    table = np.asarray(table, np.float32)
    high = table.astype(BF16)
    low = (table - high.astype(np.float32)).astype(BF16)
    return np.stack([high, low])


def split(value):
    high = value.astype(BF16)
    return high, (value - high.astype(F32)).astype(BF16)


def dot(a, b):
    return jnp.dot(a, b, preferred_element_type=F32)


def table_left(table, value):
    high, low = split(value)
    return dot(table[0], high) + (dot(table[0], low) + dot(table[1], high))


def table_right(value, table):
    high, low = split(value)
    return dot(high, table[0]) + (dot(low, table[0]) + dot(high, table[1]))


def band_tables(n, bands, points):
    half = points // 2
    slots = half // n
    keep = np.arange(half)
    keep = np.where(keep < half // 2, keep, keep - half)
    cell = np.arange(points)
    angle = 2.0 * np.pi * ((keep[:, None] * cell[None, :]) % points) / points
    cos, sin = np.cos(angle), np.sin(angle)
    top = 2.0 * np.pi * ((half // 2 * cell) % points) / points
    ctop, stop = np.cos(top), np.sin(top)
    y_out = np.concatenate([cos.T, sin.T], 1)
    y_in = np.concatenate([cos, sin], 1)
    z_out = np.block([[cos, sin], [-sin, cos]])
    z_in = np.block([[cos.T, -sin.T], [sin.T, cos.T]])
    rows = bands * half
    x_cos = np.zeros((bands, points, n, bands, slots))
    x_sin = np.zeros_like(x_cos)
    for b in range(bands):
        x_cos[b, :, :, b] = cos.T.reshape(points, n, slots)
        x_sin[b, :, :, b] = sin.T.reshape(points, n, slots)
    x_cos = x_cos.reshape(bands * points, rows)
    x_sin = x_sin.reshape(bands * points, rows)
    x_out = np.concatenate([x_cos, x_sin], 1)
    extra = np.zeros((2, 8, bands * points))
    for b in range(bands):
        extra[0, b, b * points : (b + 1) * points] = ctop
        extra[1, b, b * points : (b + 1) * points] = stop
    x_in = np.stack([np.concatenate([x_cos.T, extra[0]]), np.concatenate([x_sin.T, extra[1]])])
    ones, zeros = np.ones(points), np.zeros(points)
    point_out = np.zeros((3, points, 2 * points))
    point_in = np.zeros((3, 2 * points, points))
    for i, (c, s) in enumerate(((ones, zeros), (ctop, stop), (ones, zeros))):
        point_out[i, i + 1] = np.concatenate([c, s])
        point_out[i, half + i + 1] = np.concatenate([-s, c])
        point_in[i, :, i + 1] = np.concatenate([c, s])
        point_in[i, :, half + i + 1] = np.concatenate([-s, c])
    return [halves(t) for t in (y_out, y_in, z_out, z_in, x_out, x_in[0], x_in[1])] + [
        np.moveaxis(halves(point_out), 1, 0),
        np.moveaxis(halves(point_in), 1, 0),
        np.stack([ctop, stop]).astype(np.float32)[:, :, None],
    ]


def band_kernel(
    n, peers, bands, points, iters,
    packed, special, mask, kinetic, potential, core, rotations,
    y_out, y_in, z_out, z_in, x_out, x_in_c, x_in_s, point_out, point_in, phase, y_phase,
    new_out, special_out, density_out,
    current, applied, sent, got, grams, grams_got, levels_r, levels_i, mixed,
    special_got, part, part_got, send_sem, recv_sem, gram_send, gram_recv, first_sem, last_sem, dens_sem,
):
    me = lax.axis_index("grid")
    band = lax.axis_index("band")
    half = points // 2
    slots = half // n
    planes = points // n
    rows = bands * half
    home = n // 2
    high_owner = (half // 2) // planes

    def at(grid):
        return {"band": band, "grid": grid}

    barrier = pltpu.get_barrier_semaphore()

    @pl.loop(1, n)
    def _(i):
        pl.semaphore_signal(barrier, inc=1, device_id=at(lax.rem(me + i, n)), device_id_type=MESH)

    for i in range(1, peers):
        pl.semaphore_signal(
            barrier, inc=1, device_id={"band": lax.rem(band + i, peers), "grid": me}, device_id_type=MESH
        )
    pl.semaphore_wait(barrier, n - 1 + peers - 1)

    def plane_of(device):
        slot = device * slots
        return jnp.where(slot < half // 2, slot, slot + half)

    def first_copy(target):
        start = plane_of(target)
        return pltpu.make_async_remote_copy(
            src_ref=packed.at[:, pl.ds(lax.rem(start, planes), slots)],
            dst_ref=current,
            send_sem=first_sem.at[5 + lax.rem(start, planes) // slots],
            recv_sem=first_sem.at[1],
            device_id=at(target),
            device_id_type=MESH,
        )

    def first_own():
        return pltpu.make_async_copy(
            packed.at[:, pl.ds(lax.rem(plane_of(me), planes), slots)], current, first_sem.at[1]
        )

    def point_copy(place):
        return pltpu.make_async_remote_copy(
            src_ref=special,
            dst_ref=special_got.at[place],
            send_sem=first_sem.at[place * 2],
            recv_sem=first_sem.at[3 + place],
            device_id=at(home),
            device_id_type=MESH,
        )

    source = plane_of(me) // planes

    @pl.when(source == me)
    def _():
        first_own().start()

    @pl.loop(0, n)
    def _(target):
        @pl.when(jnp.logical_and(plane_of(target) // planes == me, target != me))
        def _():
            first_copy(target).start()

    @pl.when(me == 0)
    def _():
        point_copy(0).start()

    @pl.when(me == high_owner)
    def _():
        point_copy(1).start()

    @pl.loop(0, n)
    def _(target):
        @pl.when(jnp.logical_and(plane_of(target) // planes == me, target != me))
        def _():
            first_copy(target).wait_send()

    @pl.when(me == 0)
    def _():
        point_copy(0).wait_send()

    @pl.when(me == high_owner)
    def _():
        point_copy(1).wait_send()

    @pl.when(source == me)
    def _():
        first_own().wait()

    @pl.when(source != me)
    def _():
        first_copy(me).wait_recv()

    @pl.when(me == home)
    def _():
        point_copy(0).wait_recv()
        point_copy(1).wait_recv()
        for b in range(bands):
            current[b, 0, 0:8, :] = current[b, 0, 0:8, :] * mask[0, 0:8, :] * special[0, 8:16, :] + (
                special_got[0, b, 0:8, :] + special_got[1, b, 0:8, :]
            )

    for b in range(bands):
        current[b] = current[b] * mask[...]

    lanes = lax.broadcasted_iota(jnp.int32, (1, points), 1)
    sign = jnp.where(lanes < half, -1.0, 1.0).astype(F32)
    alone = jnp.where(lax.rem(lanes, half) == 0, 1.0, 0.0).astype(F32)

    def turn(value):
        return pltpu.roll(value, half, 1) * sign

    def exchange(stage, with_gram):
        def copies(target, origin):
            found = [
                pltpu.make_async_remote_copy(
                    src_ref=sent.at[stage, target],
                    dst_ref=got.at[stage, origin],
                    send_sem=send_sem.at[stage, target],
                    recv_sem=recv_sem.at[stage, origin],
                    device_id=at(target),
                    device_id_type=MESH,
                )
            ]
            if with_gram is not None:
                found.append(
                    pltpu.make_async_remote_copy(
                        src_ref=grams.at[with_gram],
                        dst_ref=grams_got.at[with_gram, origin],
                        send_sem=gram_send.at[with_gram, target],
                        recv_sem=gram_recv.at[with_gram, origin],
                        device_id=at(target),
                        device_id_type=MESH,
                    )
                )
            return found

        @pl.loop(1, n)
        def _(i):
            for copy in copies(lax.rem(me + i, n), me):
                copy.start()

        own = pltpu.make_async_copy(sent.at[stage, me], got.at[stage, me], recv_sem.at[stage, me])
        own.start()
        if with_gram is not None:
            mine = pltpu.make_async_copy(
                grams.at[with_gram], grams_got.at[with_gram, me], gram_recv.at[with_gram, me]
            )
            mine.start()
            mine.wait()
        own.wait()

        @pl.loop(1, n)
        def _(i):
            for copy in copies(lax.rem(me + i, n), me):
                copy.wait_send()
            origin = lax.rem(me + n - i, n)
            for copy in copies(origin, origin):
                copy.wait_recv()

    def y_outward(source_ref, stage):
        for b in range(bands):
            for x in range(slots):
                value = source_ref[b, x]
                full = table_left(y_out, jnp.concatenate([value, turn(value)], 0))
                sent[stage, :, b, x] = full.reshape(n, planes, points)

    def y_inward(stage, b, x):
        value = got[stage, :, b, x].reshape(points, points)
        return table_left(y_in, jnp.concatenate([value, -turn(value)], 0))

    def swapped(value, s):
        return jnp.concatenate([s * value[:, points:], -s * value[:, :points]], 1)

    y_phase_c = y_phase[0]
    y_phase_s = y_phase[1]

    def space(y_action):
        points_x, points_row = [], []
        for b in range(bands):
            row = mixed[home, b, 0]
            points_x.append(table_right(row, point_out[0]))
            along_z = table_right(row, point_out[1])
            along_y = table_right(row, point_out[2])
            points_row.append(along_z + along_y * y_phase_c + swapped(along_y, -1.0) * y_phase_s)
            mixed[home, b, 0] = row * alone
        levels = table_right(mixed[...].reshape(rows * planes, points), z_out)
        levels_r[0 : rows * planes, :] = levels[:, :points]
        levels_i[0 : rows * planes, :] = levels[:, points:]
        for y in range(planes):
            real = levels_r[pl.ds(y, rows, stride=planes), :]
            imag = levels_i[pl.ds(y, rows, stride=planes), :]
            stacked = jnp.concatenate(
                [jnp.concatenate([real, imag], 1), jnp.concatenate([-imag, real], 1)], 0
            )
            wave = table_left(x_out, stacked)
            found = []
            for b in range(bands):
                at_x = points_x[b][y : y + 1]
                found.append(
                    wave[b * points : (b + 1) * points]
                    + phase[0] * at_x
                    + phase[1] * swapped(at_x, -1.0)
                    + points_row[b][y : y + 1]
                )
            y_action(y, found)

    def spectrum(stage):
        def action(y, found):
            field = potential[y]
            product = jnp.concatenate([f * jnp.concatenate([field, field], 1) for f in found], 0)
            slotted = table_left(x_in_c, product) + table_left(x_in_s, swapped(product, 1.0))
            levels_r[pl.ds(y, rows + 8, stride=planes), :] = slotted[:, :points]
            levels_i[pl.ds(y, rows + 8, stride=planes), :] = slotted[:, points:]

        space(action)
        both = jnp.concatenate([levels_r[...], levels_i[...]], 1)
        found = table_right(both[0 : rows * planes], z_in).reshape(n, bands, slots, planes, points)
        sent[stage] = found
        for b in range(bands):
            start = (rows + b) * planes
            top = both[start : start + planes]
            zero = both[b * slots * planes : b * slots * planes + planes]
            last = table_right(zero, point_in[2])
            last = last * y_phase_c - turn(last) * y_phase_s
            sent[stage, home, b, 0] = (
                sent[stage, home, b, 0] * alone
                + table_right(top, point_in[0])
                + table_right(zero, point_in[1])
                + last
            )

    def pairs():
        return [(i, j) for i in range(bands) for j in range(bands)]

    def mixing(which, turn_at):
        total = jnp.sum(jnp.sum(grams_got[which], 0), 1, keepdims=True)
        square = bands * bands
        cc = {ij: total[k : k + 1] for k, ij in enumerate(pairs())}
        ca = {ij: total[square + k : square + k + 1] for k, ij in enumerate(pairs())}
        aa = {ij: total[2 * square + k : 2 * square + k + 1] for k, ij in enumerate(pairs())}
        factor = [1.0 + step_size * (ca[i, i] / (cc[i, i] + epsilon)) for i in range(bands)]
        moved = {
            (i, j): factor[i] * factor[j] * cc[i, j]
            - step_size * (factor[i] * ca[i, j] + factor[j] * ca[j, i])
            + step_size * step_size * aa[i, j]
            for i, j in pairs()
        }
        weights = []
        for b in range(bands):
            r = [rotations[turn_at, b, c] for c in range(bands)]
            length = sum(r[i] * r[j] * moved[i, j] for i, j in pairs())
            scale = lax.rsqrt(jnp.maximum(length, 0.0) + epsilon)
            weights.append([(scale * r[c] * factor[c], scale * r[c] * (-step_size)) for c in range(bands)])
        return weights

    y_outward(current, 0)
    exchange(0, None)
    mixed[...] = got[0]
    stage = 0
    for t in range(iters):
        spectrum(stage + 1)
        exchange(stage + 1, None)
        for b in range(bands):
            for x in range(slots):
                applied[b, x] = mask[x] * (
                    kinetic[x] * current[b, x] + y_inward(stage + 1, b, x) * (1.0 / points**3)
                )
        for k, (i, j) in enumerate(pairs()):
            for q, (u, v) in enumerate(((current, current), (current, applied), (applied, applied))):
                product = jnp.sum((u[i] * v[j]).reshape(slots * half, points), 0, keepdims=True)
                grams[t, q * bands * bands + k : q * bands * bands + k + 1, :] = product
        y_outward(applied, stage + 2)
        exchange(stage + 2, t)
        weights = mixing(t, t)
        old = [got[0, :, b] for b in range(bands)]
        new_mixed, new_current = [], []
        for b in range(bands):
            new_mixed.append(
                sum(weights[b][c][0] * old[c] + weights[b][c][1] * got[stage + 2, :, c] for c in range(bands))
            )
            new_current.append(
                sum(weights[b][c][0] * current[c] + weights[b][c][1] * applied[c] for c in range(bands))
            )
        for b in range(bands):
            current[b] = new_current[b]
            mixed[:, b] = new_mixed[b]
            got[0, :, b] = new_mixed[b]
        stage += 2

    def last_arrival(origin):
        place = new_out.at[:, pl.ds(lax.rem(plane_of(origin), planes), slots)]
        return pltpu.make_async_remote_copy(
            src_ref=current,
            dst_ref=place,
            send_sem=last_sem.at[0],
            recv_sem=last_sem.at[4 + lax.rem(plane_of(origin), planes) // slots],
            device_id=at(origin),
            device_id_type=MESH,
        )

    def last_sent():
        return pltpu.make_async_remote_copy(
            src_ref=current,
            dst_ref=new_out.at[:, pl.ds(lax.rem(plane_of(me), planes), slots)],
            send_sem=last_sem.at[0],
            recv_sem=last_sem.at[4 + lax.rem(plane_of(me), planes) // slots],
            device_id=at(source),
            device_id_type=MESH,
        )

    def last_own():
        return pltpu.make_async_copy(
            current, new_out.at[:, pl.ds(lax.rem(plane_of(me), planes), slots)], last_sem.at[0]
        )

    def point_back(target, sem):
        return pltpu.make_async_remote_copy(
            src_ref=current.at[:, 0, pl.ds(0, 8)],
            dst_ref=special_out,
            send_sem=last_sem.at[sem],
            recv_sem=last_sem.at[3],
            device_id=at(target),
            device_id_type=MESH,
        )

    @pl.when(source == me)
    def _():
        last_own().start()

    @pl.when(source != me)
    def _():
        last_sent().start()

    @pl.when(me == home)
    def _():
        point_back(0, 1).start()
        point_back(high_owner, 2).start()

    @pl.when(jnp.logical_and(me != 0, me != high_owner))
    def _():
        special_out[...] = jnp.zeros_like(special_out)

    @pl.when(jnp.logical_and(me * planes >= half // 2, me * planes < points - half // 2))
    def _():
        new_out[...] = jnp.zeros_like(new_out)

    def density(y, found):
        total = sum(f[:, :points] * f[:, :points] + f[:, points:] * f[:, points:] for f in found)
        part[y] = total * (2.0 / (bands * peers))
        for i in range(1, peers):
            swap(i, y).start()

    def swap(i, y):
        return pltpu.make_async_remote_copy(
            src_ref=part.at[y],
            dst_ref=part_got.at[i - 1, y],
            send_sem=dens_sem.at[0, i - 1, y],
            recv_sem=dens_sem.at[1, i - 1, y],
            device_id={"band": lax.rem(band + i, peers), "grid": me},
            device_id_type=MESH,
        )

    space(density)
    for i in range(1, peers):
        for y in range(planes):
            swap(i, y).wait()
    total = part[...] + core[...]
    for i in range(1, peers):
        total = total + part_got[i - 1]
    density_out[...] = total

    @pl.when(source == me)
    def _():
        last_own().wait()

    @pl.when(source != me)
    def _():
        last_sent().wait_send()

    @pl.when(me == home)
    def _():
        point_back(0, 1).wait_send()
        point_back(high_owner, 2).wait_send()

    @pl.when(jnp.logical_or(me == 0, me == high_owner))
    def _():
        point_back(home, 1).wait_recv()

    @pl.loop(0, n)
    def _(origin):
        @pl.when(jnp.logical_and(plane_of(origin) // planes == me, origin != me))
        def _():
            last_arrival(origin).wait_recv()


def update_bands(coefficients, potential, core, rotations):
    n, peers = lax.axis_size("grid"), lax.axis_size("band")
    bands, _, planes, points, _ = coefficients.shape
    iters = rotations.shape[0]
    half, quarter = points // 2, points // 4
    slots = half // n
    me = lax.axis_index("grid")

    def keep(value, axis):
        low = lax.slice_in_dim(value, 0, quarter, axis=axis)
        high = lax.slice_in_dim(value, points - quarter, points, axis=axis)
        return jnp.concatenate([low, high], axis)

    kept = keep(keep(coefficients, 3), 4)
    packed = jnp.concatenate([kept[:, 0], kept[:, 1]], -1)
    along_x = jnp.where(me == quarter // planes, coefficients[:, :, quarter % planes, 0, 0], 0.0)
    along_z = jnp.where(me == 0, coefficients[:, :, 0, 0, quarter], 0.0)
    along_y = jnp.where(me == 0, coefficients[:, :, 0, quarter, 0], 0.0)
    row = jnp.stack([jnp.zeros_like(along_x), along_x, along_z, along_y], -1)
    row = jnp.pad(row, ((0, 0), (0, 0), (0, half - 4))).reshape(bands, 1, points)
    lane = lax.iota(jnp.int32, points)
    zero_lane = (lane % half == 0).astype(F32)
    special = jnp.concatenate(
        [jnp.pad(row, ((0, 0), (0, 7), (0, 0))), jnp.broadcast_to(zero_lane, (bands, 8, points))], 1
    )

    def frequency(slot):
        return jnp.where(slot < quarter, slot, slot - half)

    gx = frequency(me * slots + lax.iota(jnp.int32, slots))[:, None, None]
    gy = frequency(lax.iota(jnp.int32, half))[None, :, None]
    gz = frequency(lane % half)[None, None, :]
    squared = gx * gx + gy * gy + gz * gz
    spot = (gx == -quarter) & (gy == 0) & (lane % half < 4)[None, None, :]
    squared = jnp.where(spot, quarter * quarter, squared)
    mask = (16 * squared <= points * points).astype(F32)
    kinetic = kinetic_scale * squared.astype(F32) / (points * points)

    rows = bands * half
    vmem = pl.BlockSpec(memory_space=pltpu.VMEM)
    smem = pl.BlockSpec(memory_space=pltpu.SMEM)
    stages = 2 * iters + 1
    chunk = (bands, slots, planes, points)
    gram_rows = -(-3 * bands * bands // 8) * 8
    dma = pltpu.SemaphoreType.DMA
    tables = band_tables(n, bands, points)
    y_phase = lax.dynamic_slice_in_dim(jnp.asarray(tables[-1]), me * planes, planes, 1)
    new, back, density = pl.pallas_call(
        functools.partial(band_kernel, n, peers, bands, points, iters),
        out_shape=(
            jax.ShapeDtypeStruct((bands, planes, half, points), F32),
            jax.ShapeDtypeStruct((bands, 8, points), F32),
            jax.ShapeDtypeStruct((planes, points, points), F32),
        ),
        in_specs=[vmem] * 6 + [smem] + [vmem] * (len(tables) + 1),
        out_specs=(vmem, vmem, vmem),
        scratch_shapes=[
            pltpu.VMEM((bands, slots, half, points), F32),
            pltpu.VMEM((bands, slots, half, points), F32),
            pltpu.VMEM((stages, n) + chunk, F32),
            pltpu.VMEM((stages, n) + chunk, F32),
            pltpu.VMEM((iters, gram_rows, points), F32),
            pltpu.VMEM((iters, n, gram_rows, points), F32),
            pltpu.VMEM(((rows + 8) * planes, points), F32),
            pltpu.VMEM(((rows + 8) * planes, points), F32),
            pltpu.VMEM((n,) + chunk, F32),
            pltpu.VMEM((2, bands, 16, points), F32),
            pltpu.VMEM((planes, points, points), F32),
            pltpu.VMEM((max(peers - 1, 1), planes, points, points), F32),
            dma((stages, n)),
            dma((stages, n)),
            dma((iters, n)),
            dma((iters, n)),
            dma((5 + planes // slots,)),
            dma((4 + planes // slots,)),
            dma((2, max(peers - 1, 1), planes)),
        ],
        compiler_params=pltpu.CompilerParams(
            collective_id=0, has_side_effects=True, vmem_limit_bytes=60 * 2**20
        ),
    )(packed, special, mask, kinetic, potential, core, rotations, *tables, y_phase)

    parts = jnp.stack([new[..., :half], new[..., half:]], 1)

    def widen(value, axis):
        low = lax.slice_in_dim(value, 0, quarter, axis=axis)
        high = lax.slice_in_dim(value, quarter, half, axis=axis)
        shape = list(value.shape)
        shape[axis] = points - half
        return jnp.concatenate([low, jnp.zeros(shape, F32), high], axis)

    gx_own = me * planes + lax.iota(jnp.int32, planes)
    live = (gx_own != points - quarter)[:, None, None] | (
        (lax.iota(jnp.int32, half) == 0)[None, :, None] & (lax.iota(jnp.int32, half) == 0)[None, None, :]
    )
    kept_plane = ((gx_own < quarter) | (gx_own >= points - quarter))[:, None, None]
    wide = widen(widen(jnp.where(live & kept_plane, parts, 0.0), 3), 4)
    found = back[:, 0].reshape(bands, 2, half)
    i_x = lax.broadcasted_iota(jnp.int32, (1, 1, planes, points, points), 2) + me * planes
    i_y = lax.broadcasted_iota(jnp.int32, (1, 1, planes, points, points), 3)
    i_z = lax.broadcasted_iota(jnp.int32, (1, 1, planes, points, points), 4)

    def spread(k):
        return found[:, :, k][:, :, None, None, None]

    wide = jnp.where((i_x == quarter) & (i_y == 0) & (i_z == 0), spread(1), wide)
    wide = jnp.where((i_x == 0) & (i_y == 0) & (i_z == quarter), spread(2), wide)
    wide = jnp.where((i_x == 0) & (i_y == quarter) & (i_z == 0), spread(3), wide)
    return wide, density


def frequencies(points, offset, length):
    places = offset + lax.iota(jnp.int32, length)
    return jnp.where(2 * places < points, places, places - points)


def reciprocal_tables(points, offset, length):
    along_x = frequencies(points, offset, length)
    along = frequencies(points, 0, points)
    squared = (
        along_x[:, None, None] * along_x[:, None, None]
        + along[None, :, None] * along[None, :, None]
        + along[None, None, :] * along[None, None, :]
    )
    return jnp.where(
        squared > 0, coulomb_scale * (points * points) / jnp.maximum(squared, 1).astype(F32), 0.0
    )


def full_dot(a, b):
    return jnp.dot(a, b, preferred_element_type=F32, precision=lax.Precision.HIGHEST)


def field_kernel(
    n, peers, points, hidden,
    density, cube, external, coulomb, basis, basis_2, slope_2, slope_t2, mlp_in, mlp_out, out,
    staged, sent, got, back_h, back_y, got_h, got_y, send_sem, recv_sem, share_sem,
):
    me = lax.axis_index("grid")
    band = lax.axis_index("band")
    planes = points // n
    block = planes * planes

    barrier = pltpu.get_barrier_semaphore()

    @pl.loop(1, n)
    def _(i):
        pl.semaphore_signal(
            barrier, inc=1, device_id={"band": band, "grid": lax.rem(me + i, n)}, device_id_type=MESH
        )

    share = planes // peers if planes % peers == 0 else planes
    others = range(1, peers) if share < planes else range(0)
    for i in others:
        pl.semaphore_signal(
            barrier, inc=1, device_id={"band": lax.rem(band + i, peers), "grid": me}, device_id_type=MESH
        )

    def exchange(pairs):
        def copy(k, target, origin):
            source, place = pairs[k][1:]
            return pltpu.make_async_remote_copy(
                src_ref=source.at[target],
                dst_ref=place.at[pl.ds(origin * block, block)],
                send_sem=send_sem.at[pairs[k][0], target],
                recv_sem=recv_sem.at[pairs[k][0], origin],
                device_id={"band": band, "grid": target},
                device_id_type=MESH,
            )

        @pl.loop(1, n)
        def _(i):
            for k in range(len(pairs)):
                copy(k, lax.rem(me + i, n), me).start()

        for stage, source, place in pairs:
            own = pltpu.make_async_copy(
                source.at[me], place.at[pl.ds(me * block, block)], recv_sem.at[stage, me]
            )
            own.start()
            own.wait()

        @pl.loop(1, n)
        def _(i):
            origin = lax.rem(me + n - i, n)
            for k in range(len(pairs)):
                copy(k, lax.rem(me + i, n), me).wait_send()
                copy(k, origin, origin).wait_recv()

    for y in range(planes):
        level = full_dot(full_dot(basis[...], density[y] - 2.275), basis[...])
        staged[pl.ds(y, points, stride=planes), :] = level
    sent[...] = staged[...].reshape(n, block, points)
    pl.semaphore_wait(barrier, n - 1 + len(others))
    exchange([(0, sent, got)])
    arrived = got[...].reshape(n, planes, planes, points)
    for x in range(planes):
        column = arrived[:, x].reshape(points, points)
        weighted = coulomb[x] * full_dot(basis[...], column)
        back_h[:, x * planes : (x + 1) * planes] = table_left(basis_2, weighted).reshape(n, planes, points)
        back_y[:, x * planes : (x + 1) * planes] = table_left(slope_2, column).reshape(n, planes, points)
    exchange([(1, back_h, got_h), (2, back_y, got_y)])

    def shared(other, whose, i):
        part = out.at[whose * share + i]
        return pltpu.make_async_remote_copy(
            src_ref=part,
            dst_ref=part,
            send_sem=share_sem.at[0, other - 1, i],
            recv_sem=share_sem.at[1, other - 1, i],
            device_id={"band": lax.rem(band + other, peers), "grid": me},
            device_id_type=MESH,
        )

    first = band * share if share < planes else 0
    for i in range(share):
        y = first + i
        both = jnp.concatenate(
            [got_h[pl.ds(y, points, stride=planes), :], got_y[pl.ds(y, points, stride=planes), :]], 1
        )
        both = table_left(basis_2, both)
        both = table_right(jnp.concatenate([both[:, :points], both[:, points:]], 0), basis_2)
        hartree = both[:points]
        change_y = both[points:] * (1.0 / (points * points))
        varying = density[y] - 2.275
        change_x = table_left(slope_2, varying)
        change_z = table_right(varying, slope_t2)
        gradient = jnp.sqrt(change_x * change_x + change_y * change_y + change_z * change_z)
        root = cube[y]
        reduced = gradient / (reduced_scale * density[y] * root)
        bounded = reduced / (1.0 + reduced)

        def unit(k, total):
            return total + mlp_out[k] * jnp.tanh(mlp_in[0, k] * root + mlp_in[1, k] * bounded + mlp_in[2, k])

        enhance = lax.fori_loop(0, hidden, unit, jnp.ones_like(root), unroll=4)
        out[y] = external[y] + hartree - exchange_scale * root * enhance
        for other in others:
            shared(other, band, i).start()

    for other in others:
        for i in range(share):
            shared(other, band, i).wait_send()
            shared(other, lax.rem(band + peers - other, peers), i).wait_recv()


def body(coefficients, potential, external, core_density, rotations, mlp_in, mlp_out):
    points = potential.shape[1]
    planes = coefficients.shape[2]
    n, peers = lax.axis_size("grid"), lax.axis_size("band")
    offset = lax.axis_index("grid") * planes
    coulomb = reciprocal_tables(points, offset, planes) * (1.0 / points**3)
    current, density = update_bands(coefficients, potential, core_density, rotations)

    cell = np.arange(points)
    angle = 2.0 * np.pi * ((cell[:, None] * cell[None, :]) % points) / points
    freq = np.where(2 * cell < points, cell, cell - points)
    slope = gradient_scale * np.where(2 * freq == -points, 0, freq) / points
    back = (np.exp(1j * angle) * slope[None, :] * 1j) @ np.exp(-1j * angle) / points
    slope_table = np.ascontiguousarray(back.real).astype(np.float32)
    basis = (np.cos(angle) + np.sin(angle)).astype(np.float32)
    vmem = pl.BlockSpec(memory_space=pltpu.VMEM)
    smem = pl.BlockSpec(memory_space=pltpu.SMEM)
    block = planes * planes
    new_potential = pl.pallas_call(
        functools.partial(field_kernel, n, peers, points, mlp_out.shape[0]),
        out_shape=jax.ShapeDtypeStruct((planes, points, points), F32),
        in_specs=[vmem] * 8 + [smem, smem],
        out_specs=vmem,
        scratch_shapes=[
            pltpu.VMEM((n * block, points), F32),
            pltpu.VMEM((n, block, points), F32),
            pltpu.VMEM((n * block, points), F32),
            pltpu.VMEM((n, block, points), F32),
            pltpu.VMEM((n, block, points), F32),
            pltpu.VMEM((n * block, points), F32),
            pltpu.VMEM((n * block, points), F32),
            pltpu.SemaphoreType.DMA((3, n)),
            pltpu.SemaphoreType.DMA((3, n)),
            pltpu.SemaphoreType.DMA((2, max(peers - 1, 1), planes)),
        ],
        compiler_params=pltpu.CompilerParams(
            collective_id=1, has_side_effects=True, vmem_limit_bytes=40 * 2**20
        ),
    )(
        density, jnp.cbrt(density), external, coulomb, basis,
        halves(basis), halves(slope_table), halves(slope_table.T), mlp_in, mlp_out,
    )
    return (current, new_potential)


def solution(mesh):
    in_specs = (
        P("band", None, "grid", None, None),
        P("grid", None, None),
        P("grid", None, None),
        P("grid", None, None),
        P(None, "band", None),
        P(),
        P(),
    )
    out_specs = (P("band", None, "grid", None, None), P("grid", None, None))
    return jax.shard_map(body, mesh=mesh, in_specs=in_specs, out_specs=out_specs, check_vma=False)
```

profile of v0, /device:TPU:29, one launch (start us, length us, event | category | flops | bytes accessed | tf_op | source)
XLA Modules:
  0.0 179.1 jit_solution(2215348997629260736)
XLA Ops:
  0.7 0.1 pad.11.clone
  0.8 0.1 broadcast_and_fusion.1
  0.9 0.1 broadcast_add_fusion.1
  1.0 1.0 fusion.10
  2.0 0.1 pad_maximum_fusion.4
  2.1 0.1 copy.44
  2.2 0.1 reshape.281
  2.3 0.1 broadcast_add_fusion
  2.3 0.6 select_maximum_fusion.special
  2.9 0.1 broadcast_and_fusion
  3.0 1.3 constant_dynamic-slice_fusion.y_phase
  4.3 0.1 or_and_fusion
  4.4 0.8 convert_multiply_fusion.kinetic
  5.2 0.8 fusion.9.mask
  6.0 0.3 and_and_fusion.2
  6.3 0.2 fusion.5.coulomb
  6.6 1.3 fusion.22
  7.8 0.4 slice_maximum_fusion
  8.2 0.3 fusion.7
  8.6 1.0 pad_maximum_fusion.3.packed
  9.6 0.0 copy-start.1
  9.6 0.0 copy-start.2
  9.6 0.0 copy-start.3
  9.6 0.0 copy-start.4
  9.6 0.0 copy-start.5
  9.6 0.0 copy-start.6
  9.6 0.0 copy-start.7
  9.6 112.5 %shard_map.212 = (f32[2,8,64,128]{3,2,1,0:T(8,128)}, f32[2,8,128]{2,1,0:T(8,128)}, f32[8,128,128]{2,1,0:T(8,128)}) custom-call(f32[2,8,64,128]{3,2,1,0:T(8,128)} %pad_maximum_fusion.3.packed, f32[2,16,128]{2,1,0:T(8,128)} %select_maximum_fusion.special, f32[4,64,128]{2,1,0:T(8,128)} %fusion.9.mask, f32[4,64,128]{2,1,0:T(8,128)} %convert_multiply_fusion.kinetic, ...), custom_call_target="tpu_custom_call" | custom-call | tf_op jit(solution)/shard_map/pallas_call | solution.py:549
  122.1 0.0 copy-start.8
  122.1 0.8 slice_reduce_fusion
  122.9 0.1 reshape_squeeze.3
  123.0 0.1 fusion.24
  123.1 0.1 copy.41
  123.2 0.1 copy.42
  123.3 0.1 copy.43
  123.4 1.4 cbrt.3.cube
  124.8 0.0 copy-done.1
  124.8 0.0 copy-done.2
  124.8 0.0 copy-done.3
  124.8 0.0 copy-done.4
  124.8 0.0 copy-done.5
  124.9 0.0 copy-done.6
  124.9 0.0 copy-done.7
  124.9 0.0 copy-start
  124.9 1.0 copy-done
  125.9 48.8 %shard_map.213 = f32[8,128,128]{2,1,0:T(8,128)S(1)} custom-call(f32[8,128,128]{2,1,0:T(8,128)S(1)} %copy-done, f32[8,128,128]{2,1,0:T(8,128)S(1)} %cbrt.3.cube, f32[8,128,128]{2,1,0:T(8,128)S(1)} %copy-done.1, f32[8,128,128]{2,1,0:T(8,128)S(1)} %fusion.5.coulomb, f32[128,128]{1,0:T(8,128)S(1)} %copy-done.5, bf16[2,128,128]{2,1,0:T(8,128)(2,1)S(1)} %copy-done.4, ...), custom_call_target="tpu_custom_call" | custom-call | tf_op jit(solution)/shard_map/pallas_call | solution.py:766
  174.7 0.0 copy-done.8
  174.7 0.2 slice_bitcast_fusion.1
  174.9 0.2 maximum_select_fusion.1
  175.1 0.1 fusion.23
  175.2 0.1 broadcast_in_dim.95
  175.3 0.2 pad_maximum_fusion
  175.4 0.7 fusion.21
  176.2 2.1 %fusion.1 = f32[2,2,8,128,128]{4,3,2,1,0:T(8,128)} fusion(f32[128]{0:T(128)S(1)} %pad.11.clone, f32[2,2]{1,0:T(2,128)S(1)} %bitcast.20, f32[2,2]{1,0:T(2,128)S(1)} %bitcast.19, f32[2,2]{1,0:T(2,128)S(1)} %bitcast.18, pred[8,128,128]{2,1,0:T(8,128)(4,1)S(1)} %get-tuple-element.28, pred[8,128,128]{2,1,0:T(8,128)(4,1)S(1)} %get-tuple-element.27, ...), kind=kLoop, calls=%fused_computation.3 | loop fusion | flops 2621440 | bytes 3539504 | tf_op jit(solution)/shard_map/jit(_where)/select_n | solution.py:609
  178.3 0.8 copy.57
  (17 shorter events, 0.1 us)
Async XLA Ops:
  9.6 115.2 %copy-start.1 = (f32[8,128,128]{2,1,0:T(8,128)S(1)}, f32[8,128,128]{2,1,0:T(8,128)}, u32[]{:S(2)}) copy-start(f32[8,128,128]{2,1,0:T(8,128)} %external.1) | copy-start | bytes 1572868
  9.6 115.2 %copy-start.2 = (bf16[2,128,128]{2,1,0:T(8,128)(2,1)S(1)}, bf16[2,128,128]{2,1,0:T(8,128)(2,1)}, u32[]{:S(2)}) copy-start(bf16[2,128,128]{2,1,0:T(8,128)(2,1)} %constant.131.clone.slope_t2) | copy-start | bytes 196612
  9.6 115.2 %copy-start.3 = (bf16[2,128,128]{2,1,0:T(8,128)(2,1)S(1)}, bf16[2,128,128]{2,1,0:T(8,128)(2,1)}, u32[]{:S(2)}) copy-start(bf16[2,128,128]{2,1,0:T(8,128)(2,1)} %constant.130.clone.slope_2) | copy-start | bytes 196612
  9.6 115.3 %copy-start.4 = (bf16[2,128,128]{2,1,0:T(8,128)(2,1)S(1)}, bf16[2,128,128]{2,1,0:T(8,128)(2,1)}, u32[]{:S(2)}) copy-start(bf16[2,128,128]{2,1,0:T(8,128)(2,1)} %constant.129.clone.basis_2) | copy-start | bytes 196612
  9.6 115.3 %copy-start.5 = (f32[128,128]{1,0:T(8,128)S(1)}, f32[128,128]{1,0:T(8,128)}, u32[]{:S(2)}) copy-start(f32[128,128]{1,0:T(8,128)} %constant.128.clone.basis) | copy-start | bytes 196612
  9.6 115.3 %copy-start.6 = (f32[3,32]{1,0:T(4,128)S(1)}, f32[3,32]{1,0:T(4,128)}, u32[]{:S(2)}) copy-start(f32[3,32]{1,0:T(4,128)} %mlp_in.1) | copy-start | bytes 1156
  9.6 115.3 %copy-start.7 = (f32[32]{0:T(128)S(1)}, f32[32]{0:T(128)}, u32[]{:S(2)}) copy-start(f32[32]{0:T(128)} %mlp_out.1) | copy-start | bytes 388
  122.1 52.6 %copy-start.8 = (f32[2,8,64,128]{3,2,1,0:T(8,128)S(1)}, f32[2,8,64,128]{3,2,1,0:T(8,128)}, u32[]{:S(2)}) copy-start(f32[2,8,64,128]{3,2,1,0:T(8,128)} %get-tuple-element.6) | copy-start | bytes 1572868
  124.9 1.0 copy-start
where the time goes:
time: 179 us
  Pallas kernels  161 us (90%)
  local copies, waits for them, and re-layouts  8.52 us (5%)
  other arithmetic  8.39 us (5%)
    pallas_call x1, Pallas kernels, update_bands(): pl.pallas_call(functools.partial(band_kernel, n, peers, bands, points, it...  112 us
    pallas_call x1, Pallas kernels, body(): pl.pallas_call(functools.partial(field_kernel, n, peers, points, mlp_out....  48.8 us

commit v1 on v0

v1 whole, which is shorter than its diff:
```python
import functools
import math

import jax
import jax.numpy as jnp
import numpy as np
from jax import lax
from jax.experimental import pallas as pl
from jax.experimental.pallas import tpu as pltpu
from jax.sharding import PartitionSpec as P

MESH = pl.DeviceIdType.MESH
F32 = jnp.float32
BF16 = jnp.bfloat16
HIGHEST = lax.Precision.HIGHEST

step_size = 0.2
epsilon = 1e-06
spacing = 0.58
kinetic_scale = 0.5 * (2.0 * math.pi / spacing) ** 2
coulomb_scale = spacing * spacing / math.pi
gradient_scale = 2.0 * math.pi / spacing
reduced_scale = 2.0 * (3.0 * math.pi * math.pi) ** (1.0 / 3.0)
exchange_scale = (3.0 / math.pi) ** (1.0 / 3.0)
level_shift = 2.275


def halves(table):
    table = np.asarray(table, np.float32)
    high = table.astype(BF16)
    low = (table - high.astype(np.float32)).astype(BF16)
    return high, low


def table_for_left(table):
    high, low = halves(table)
    return np.concatenate([high, high, low], 1)


def table_for_right(table):
    high, low = halves(table)
    return np.concatenate([high, high, low], 0)


def split(value):
    high = value.astype(BF16)
    return high, (value - high.astype(F32)).astype(BF16)


def dot(a, b):
    return jnp.dot(a, b, preferred_element_type=F32)


def left(table, value):
    high, low = split(value)
    return dot(table, jnp.concatenate([high, low, high], 0))


def right(value, table):
    high, low = split(value)
    return dot(jnp.concatenate([high, low, high], 1), table)


def full_dot(a, b):
    return jnp.dot(a, b, preferred_element_type=F32, precision=HIGHEST)


def slot_planes(n, points):
    planes, slots = points // n, points // 2 // n
    found = []
    for device in range(n):
        quarter = device // (n // 4)
        owner = device + (0, -(n // 4), n // 4, 0)[quarter]
        start = owner * planes + (0, slots, slots, 0)[quarter]
        found += [start + i for i in range(slots)]
    return np.array(found)


def cell_order(count, share):
    return np.array([o * share + k for k in range(share) for o in range(count)])


def transform_tables(n, points, count, share):
    half = points // 2
    keep = np.arange(half)
    keep = np.where(keep < half // 2, keep, keep - half)
    cell = np.arange(points)

    def waves(freq):
        angle = 2.0 * np.pi * ((freq[:, None] * cell[None, :]) % points) / points
        return np.cos(angle), np.sin(angle)

    cos, sin = waves(keep)
    plane = slot_planes(n, points)
    cos_x, sin_x = waves(np.where(2 * plane < points, plane, plane - points))
    freq = np.where(2 * cell < points, cell, cell - points)
    slope = gradient_scale * np.where(2 * freq == -points, 0, freq) / points
    cos_all, sin_all = waves(cell)
    derivative = ((cos_all + 1j * sin_all) * slope[None, :] * 1j) @ (cos_all - 1j * sin_all) / points
    derivative = derivative.real
    basis = cos_all + sin_all
    order = cell_order(count, share)
    lefts = np.stack([
        table_for_left(t) for t in (
            np.concatenate([cos.T, sin.T], 1),
            np.concatenate([cos, sin], 0),
            np.concatenate([cos_x.T, sin_x.T], 1),
            np.concatenate([cos_x, sin_x], 0),
            basis[order],
            derivative[order][:, order],
            basis[:, order],
            derivative,
        )
    ])
    rights = np.concatenate([table_for_right(basis), table_for_right(derivative.T)], 1)
    z_out = table_for_right(np.block([[cos, sin], [-sin, cos]]))
    z_in = table_for_right(np.block([[cos.T, -sin.T], [sin.T, cos.T]]))
    plain = np.stack([basis, basis[:, order]]).astype(np.float32)
    return lefts, rights, z_out, z_in, plain


def kernel(
    n, peers, bands, points, iters, hidden,
    coefficients, potential_in, external_in, core_in, rotations, mlp_in, mlp_out,
    lefts, rights, z_out, z_in, plain,
    new_out, out,
    given, potential, external, core, raw, forward, vectors, mask, kinetic,
    sent, got, level_r, level_i, edge_r, edge_i, space_of, fixed_out, fixed_got,
    gram_tile, gram_got, fresh, returned, fixed_new, fixed_back,
    parts, coulomb, staged, arrived, slope_sent, slope_got, wave_sent, wave_got, change, network,
    load_sem, first_sem, fixed_sem, send_sem, recv_sem, gram_sem, last_sem, back_sem, dens_sem, field_sem, own_sem,
    share_sem,
):
    me = lax.axis_index("grid")
    band = lax.axis_index("band")
    half = points // 2
    reach = half // 2
    slots = half // n
    planes = points // n
    zone = n // 4
    home = n - zone
    edge = home * slots
    sub = math.gcd(peers, planes)
    share = planes // sub
    count = n * sub
    block = share * share
    seat = lax.rem(band, sub)
    team = band - seat
    rank = me * sub + seat
    holder = jnp.logical_or(me < zone, me >= home)
    partner = jnp.where(
        me < zone, me + zone, jnp.where(me < 2 * zone, me - zone, jnp.where(me < home, me + zone, me - zone))
    )

    def at(grid, other=None):
        return {"band": band if other is None else other, "grid": grid}

    def remote(source, target, send, recv, device):
        return pltpu.make_async_remote_copy(
            src_ref=source, dst_ref=target, send_sem=send, recv_sem=recv, device_id=device, device_id_type=MESH
        )

    def drained(ref, sem):
        pltpu.make_async_copy(ref, ref, sem).wait()

    loads = []
    for b in range(bands):
        for p in range(2):
            k = 2 * (2 * b + p)
            loads.append(pltpu.make_async_copy(
                coefficients.at[b, p, :, pl.ds(0, reach + 8)], given.at[b, p, :, pl.ds(0, reach + 8)], load_sem.at[k]
            ))
            loads.append(pltpu.make_async_copy(
                coefficients.at[b, p, :, pl.ds(points - reach, reach)],
                given.at[b, p, :, pl.ds(reach + 8, reach)],
                load_sem.at[k + 1],
            ))
    base = 4 * bands
    late = [
        pltpu.make_async_copy(potential_in, potential, load_sem.at[base]),
        pltpu.make_async_copy(external_in, external, load_sem.at[base + 1]),
        pltpu.make_async_copy(core_in, core, load_sem.at[base + 2]),
    ]
    for copy in loads + late:
        copy.start()

    barrier = pltpu.get_barrier_semaphore()

    @pl.loop(1, count)
    def _(i):
        other = lax.rem(rank + i, count)
        pl.semaphore_signal(barrier, inc=1, device_id=at(other // sub, team + lax.rem(other, sub)), device_id_type=MESH)

    for i in range(1, peers):
        other = lax.rem(band + i, peers)

        @pl.when(other - lax.rem(other, sub) != team)
        def _():
            pl.semaphore_signal(barrier, inc=1, device_id=at(me, other), device_id_type=MESH)

    lanes = lax.broadcasted_iota(jnp.int32, (1, points), 1)
    tile_lane = lax.broadcasted_iota(jnp.int32, (8, points), 1)
    tile_row = lax.broadcasted_iota(jnp.int32, (8, points), 0)
    sign = jnp.where(lanes < half, -1.0, 1.0).astype(F32)
    alone = jnp.where(lax.rem(lanes, half) == 0, 1.0, 0.0).astype(F32)

    def quarter_turn(k):
        k = lax.rem(k, 4)
        c = jnp.where(k == 0, 1.0, jnp.where(k == 2, -1.0, 0.0)).astype(F32)
        s = jnp.where(k == 1, 1.0, jnp.where(k == 3, -1.0, 0.0)).astype(F32)
        return c, s

    z_c, z_s = quarter_turn(lanes)
    y_c, y_s = quarter_turn(me * planes + lax.broadcasted_iota(jnp.int32, (planes, 1), 0))

    def turn(value):
        return pltpu.roll(value, half, 1) * sign

    def frequency(place):
        return jnp.where(2 * place < points, place, place - points)

    own_start = jnp.where(holder, me * planes, partner * planes + slots)
    row = lax.broadcasted_iota(jnp.int32, (half, points), 0)
    gy = jnp.where(row < reach, row, row - half)
    lane = lax.rem(lax.broadcasted_iota(jnp.int32, (half, points), 1), half)
    gz = jnp.where(lane < reach, lane, lane - half)
    flat = gy * gy + gz * gz
    for x in range(slots):
        gx = frequency(own_start + x)
        squared = flat + gx * gx
        if x == 0:
            spot = jnp.logical_and(jnp.logical_and(row == 0, lane < 4), me == home)
            squared = jnp.where(spot, reach * reach, squared)
        mask[x] = jnp.where(16 * squared <= points * points, 1.0, 0.0).astype(F32)
        kinetic[x] = kinetic_scale * squared.astype(F32) / (points * points)
    edge_r[...] = jnp.zeros_like(edge_r)
    edge_i[...] = jnp.zeros_like(edge_i)

    for copy in loads:
        copy.wait()

    def packed(b, x):
        found = []
        for p in range(2):
            found.append(jnp.concatenate([given[b, p, x, 0:reach], given[b, p, x, reach + 8 : half + 8]], 0))
        real, imag = found
        low = jnp.where(lanes < reach, real, pltpu.roll(real, half, 1))
        high = jnp.where(lanes < half + reach, pltpu.roll(imag, half, 1), imag)
        return jnp.where(lanes < half, low, high)

    @pl.when(holder)
    def _():
        for b in range(bands):
            for x in range(slots):
                forward[b, x] = packed(b, slots + x)
                raw[b, x] = packed(b, x)

    def lane_to(value, start, target):
        moved = pltpu.roll(value, (target - start) % points, 1)
        return jnp.where(jnp.logical_and(tile_lane == target, tile_row == 0), moved, 0.0)

    @pl.when(me == 0)
    def _():
        for b in range(bands):
            total = None
            for p in range(2):
                z_point = lane_to(given[b, p, 0, 0:8], reach, 2 + half * p)
                y_point = lane_to(given[b, p, 0, reach : reach + 8], 0, 3 + half * p)
                total = z_point + y_point if total is None else total + z_point + y_point
            fixed_out[b] = total

    @pl.when(me == zone)
    def _():
        for b in range(bands):
            fixed_out[b] = lane_to(given[b, 0, 0, 0:8], 0, 1) + lane_to(given[b, 1, 0, 0:8], 0, 1 + half)

    pl.semaphore_wait(barrier, count - 1 + peers - sub)

    def first(b):
        return remote(forward.at[b], raw.at[b], first_sem.at[0, b], first_sem.at[1, b], at(partner))

    def fixed(place):
        return remote(fixed_out, fixed_got.at[place], fixed_sem.at[0], fixed_sem.at[1 + place], at(home))

    @pl.when(holder)
    def _():
        for b in range(bands):
            first(b).start()

    @pl.when(me == 0)
    def _():
        fixed(0).start()

    @pl.when(me == zone)
    def _():
        fixed(1).start()

    def exchange(place):
        def copy(target):
            return remote(
                sent.at[place, target], got.at[place, me], send_sem.at[place], recv_sem.at[place], at(target)
            )

        @pl.loop(1, n)
        def _(i):
            copy(lax.rem(me + i, n)).start()

        pltpu.make_async_copy(sent.at[place, me], got.at[place, me], recv_sem.at[place]).start()

    def received(place):
        drained(got.at[place], recv_sem.at[place])

    def outward(value_of, place):
        stacked = []
        for x in range(slots):
            value = value_of(x)
            stacked.append(jnp.concatenate([value, turn(value)], 0))
        full = left(lefts[0], jnp.concatenate(stacked, 1))
        for x in range(slots):
            sent[place, :, x] = full[:, x * points : (x + 1) * points].reshape(n, planes, points)
        exchange(place)

    def space(place, action):
        levels = right(got[place].reshape(half * planes, points), z_out[...])
        level_r[...] = levels[:, :points]
        level_i[...] = levels[:, points:]
        special = got[place, home, 0]

        def lane_of(k):
            return jnp.broadcast_to(special[:, k : k + 1], (planes, points))

        minus_r, plus_r, z_r, y_r = [lane_of(k) for k in range(4)]
        minus_i, plus_i, z_i, y_i = [lane_of(half + k) for k in range(4)]
        level_r[edge * planes : (edge + 1) * planes, :] = minus_r + plus_r
        level_i[edge * planes : (edge + 1) * planes, :] = minus_i + plus_i
        level_r[0:planes, :] += z_r * z_c - z_i * z_s + y_r * y_c - y_i * y_s
        level_i[0:planes, :] += z_r * z_s + z_i * z_c + y_r * y_s + y_i * y_c
        edge_r[pl.ds(0, planes, stride=8), :] = 2.0 * plus_r
        edge_i[pl.ds(0, planes, stride=8), :] = 2.0 * plus_i

        def without(value, y, extra):
            tile = value[edge : edge + 8] - extra[y * 8 : y * 8 + 8, :]
            return jnp.concatenate([value[:edge], tile, value[edge + 8 :]], 0)

        for y in range(planes):
            real = level_r[pl.ds(y, half, stride=planes), :]
            imag = level_i[pl.ds(y, half, stride=planes), :]
            stacked = jnp.concatenate(
                [
                    jnp.concatenate([real, imag], 1),
                    jnp.concatenate([-without(imag, y, edge_i), without(real, y, edge_r)], 1),
                ],
                0,
            )
            action(y, left(lefts[2], stacked))

    def spectrum(index, place):
        def action(y, wave):
            space_of[index, y] = wave
            field = potential[y]
            product = wave * jnp.concatenate([field, field], 1)
            both = left(lefts[3], product)
            cos_r, cos_i = both[:half, :points], both[:half, points:]
            sin_r, sin_i = both[half:, :points], both[half:, points:]
            level_r[pl.ds(y, half, stride=planes), :] = cos_r + sin_i
            level_i[pl.ds(y, half, stride=planes), :] = cos_i - sin_r
            edge_r[8 * (planes + y) : 8 * (planes + y) + 8, :] = cos_r[edge : edge + 8] - sin_i[edge : edge + 8]
            edge_i[8 * (planes + y) : 8 * (planes + y) + 8, :] = cos_i[edge : edge + 8] + sin_r[edge : edge + 8]

        space(place, action)
        both = jnp.concatenate([level_r[...], level_i[...]], 1)
        sent[place + bands] = right(both, z_in[...]).reshape(n, slots, planes, points)

        def total(value):
            return jnp.sum(value, 1, keepdims=True)

        plus_r = edge_r[pl.ds(8 * planes, planes, stride=8), :]
        plus_i = edge_i[pl.ds(8 * planes, planes, stride=8), :]
        zero_r, zero_i = level_r[0:planes, :], level_i[0:planes, :]
        line_r, line_i = total(zero_r), total(zero_i)
        found = [
            total(plus_r), total(zero_r * z_c + zero_i * z_s), line_r * y_c + line_i * y_s,
            total(plus_i), total(zero_i * z_c - zero_r * z_s), line_i * y_c - line_r * y_s,
        ]
        special = sent[place + bands, home, 0] * alone
        for k, value in enumerate(found):
            special = jnp.where(lanes == (k + 1 if k < 3 else half + k - 2), value, special)
        sent[place + bands, home, 0] = special
        exchange(place + bands)

    def inward(place):
        columns = [got[place, :, x].reshape(points, points) for x in range(slots)]
        both = left(lefts[1], jnp.concatenate(columns, 1))
        found = []
        for x in range(slots):
            part = both[:, x * points : (x + 1) * points]
            found.append(part[:half] - turn(part[half:]))
        return found

    grams = {}

    def measure(p):
        for q in range(p + 1):
            u = vectors[p // bands, p % bands].reshape(slots * half, points)
            v = vectors[q // bands, q % bands].reshape(slots * half, points)
            grams[q, p] = jnp.sum(u * v, 0, keepdims=True)

    for b in range(bands):
        @pl.when(jnp.logical_not(holder))
        def _():
            first(b).wait_recv()

        if b == 0:
            @pl.when(me == home)
            def _():
                fixed(0).wait_recv()
                fixed(1).wait_recv()
                for c in range(bands):
                    fixed_got[0, c] = fixed_got[0, c] + fixed_got[1, c]

        @pl.when(me == home)
        def _():
            clean = jnp.where(tile_row == 0, alone, 1.0)
            raw[b, 0, 0:8, :] = raw[b, 0, 0:8, :] * clean * mask[0, 0:8, :] + fixed_got[0, b]

        vectors[0, b] = raw[b] * mask[...]
        outward(lambda x: vectors[0, b, x], b)

    late[0].wait()
    size = (iters + 1) * bands
    for b in range(bands):
        measure(b)
    for t in range(iters):
        for b in range(bands):
            received(2 * t * bands + b)
            spectrum(t * bands + b, 2 * t * bands + b)
        for b in range(bands):
            place = (2 * t + 1) * bands + b
            received(place)
            found = inward(place)
            for x in range(slots):
                vectors[t + 1, b, x] = mask[x] * (
                    kinetic[x] * vectors[t, b, x] + found[x] * (1.0 / points**3)
                )
            last = (t + 1) * bands + b == size - 1
            if last:
                measure(size - 1)
                tile = jnp.zeros((1, points), F32)
                keys = sorted(grams)
                for k, key in enumerate(keys):
                    tile = jnp.where(lanes == k, jnp.sum(grams[key], 1, keepdims=True), tile)
                gram_tile[...] = tile

                def gram_copy(target):
                    return remote(gram_tile, gram_got.at[me], gram_sem.at[0], gram_sem.at[1], at(target))

                @pl.loop(1, n)
                def _(i):
                    gram_copy(lax.rem(me + i, n)).start()

                pltpu.make_async_copy(gram_tile, gram_got.at[me], gram_sem.at[1]).start()
            outward(lambda x: vectors[t + 1, b, x], (2 * t + 2) * bands + b)
            if not last:
                measure((t + 1) * bands + b)

    drained(gram_got, gram_sem.at[1])
    sums = jnp.sum(gram_got[...], 0)
    gram = {}
    for k, (p, q) in enumerate(keys):
        gram[p, q] = gram[q, p] = sums[:, k : k + 1]

    def product(u, v):
        total = None
        for p, a in enumerate(u):
            inner = None
            for q, c in enumerate(v):
                if a is not None and c is not None:
                    term = c * gram[p, q]
                    inner = term if inner is None else inner + term
            if inner is not None:
                total = a * inner if total is None else total + a * inner
        return total

    def combine(terms):
        result = []
        for p in range(size):
            value = None
            for scale, u in terms:
                if u[p] is not None:
                    value = scale * u[p] if value is None else value + scale * u[p]
            result.append(value)
        return result

    one = jnp.ones((1, 1), F32)
    current = [[one if p == b else None for p in range(size)] for b in range(bands)]
    for t in range(iters):
        moved = []
        for b in range(bands):
            pushed = [None] * bands + current[b][: size - bands]
            factor = 1.0 + step_size * (product(current[b], pushed) / (product(current[b], current[b]) + epsilon))
            moved.append(combine([(factor, current[b]), (-step_size, pushed)]))
        following = []
        for b in range(bands):
            rotated = combine([(rotations[t, b, c], moved[c]) for c in range(bands)])
            scale = lax.rsqrt(jnp.maximum(product(rotated, rotated), 0.0) + epsilon)
            following.append([None if value is None else scale * value for value in rotated])
        current = following

    for b in range(bands):
        for x in range(slots):
            fresh[b, x] = sum(current[b][p] * vectors[p // bands, p % bands, x] for p in range(size))

    place = 2 * iters * bands
    for b in range(bands - 1):
        received(place + b)

        def keep(y, wave):
            space_of[iters * bands + b, y] = wave

        space(place + b, keep)

    for y in range(planes):
        for b in range(bands):
            known = [space_of[p, y] for p in range(size - 1)]
            mixed = [sum(current[b][p] * known[p] for p in range(size - 1)) for b in range(bands)]
        for b in range(bands):
            space_of[b, y] = mixed[b]

    def density_copy(i, y):
        target = lax.rem(band + i, peers)
        return remote(
            parts.at[band, y], parts.at[band, y], dens_sem.at[0, i - 1, y], dens_sem.at[1, i - 1, y], at(me, target)
        )

    received(place + bands - 1)

    def density(y, wave):
        total = None
        for b in range(bands):
            value = space_of[b, y] + current[b][size - 1] * wave
            square = value * value
            square = square[:, :points] + square[:, points:]
            total = square if total is None else total + square
        parts[band, y] = total * (2.0 / (bands * peers))
        for i in range(1, peers):
            @pl.when(lax.rem(lax.rem(band + i, peers), sub) == y // share)
            def _():
                density_copy(i, y).start()

    space(place + bands - 1, density)

    late[2].wait()
    late[1].wait()
    for i in range(1, peers):
        for y in range(planes):
            @pl.when(lax.rem(lax.rem(band + i, peers), sub) == y // share)
            def _():
                density_copy(i, y).wait_send()

            @pl.when(seat == y // share)
            def _():
                density_copy(i, y).wait_recv()

    first_plane = seat * share
    whole = []
    for k in range(share):
        total = core[first_plane + k]
        for other in range(peers):
            total = total + parts[other, first_plane + k]
        whole.append(total)
    varying = [value - level_shift for value in whole]

    def field_exchange(stage, source, target):
        def copy(other):
            return remote(
                source.at[pl.ds(other * block, block)],
                target.at[pl.ds(rank * block, block)],
                field_sem.at[0, stage],
                field_sem.at[1, stage],
                at(other // sub, team + lax.rem(other, sub)),
            )

        @pl.loop(1, count)
        def _(i):
            copy(lax.rem(rank + i, count)).start()

        pltpu.make_async_copy(
            source.at[pl.ds(rank * block, block)], target.at[pl.ds(rank * block, block)], field_sem.at[1, stage]
        ).start()

    level = full_dot(plain[0], jnp.concatenate(varying, 1))
    level = jnp.concatenate([level[:, k * points : (k + 1) * points] for k in range(share)], 0)
    level = full_dot(level, plain[0])
    for k in range(share):
        staged[pl.ds(k, points, stride=share), :] = level[k * points : (k + 1) * points]
    field_exchange(0, staged, arrived)

    def last(b):
        return remote(fresh.at[b], returned.at[b], last_sem.at[0, b], last_sem.at[1, b], at(partner))

    def back(target, sem):
        return remote(fixed_new, fixed_back, back_sem.at[sem], back_sem.at[2], at(target))

    @pl.when(jnp.logical_not(holder))
    def _():
        for b in range(bands):
            last(b).start()

    @pl.when(me == home)
    def _():
        for b in range(bands):
            fixed_new[b] = fresh[b, 0, 0:8, :]
        back(0, 0).start()
        back(zone, 1).start()

    columns = jnp.concatenate(varying, 1)
    change_x = left(lefts[7], columns)
    change_z = right(jnp.concatenate(varying, 0), rights[:, points:])
    for k in range(share):
        cx = change_x[:, k * points : (k + 1) * points]
        cz = change_z[k * points : (k + 1) * points]
        change[k] = cx * cx + cz * cz
    row = lax.broadcasted_iota(jnp.int32, (points, points), 0)
    lane = lax.broadcasted_iota(jnp.int32, (points, points), 1)
    gy, gz = frequency(row), frequency(lane)
    flat = gy * gy + gz * gz
    for i in range(share):
        gx = frequency(rank * share + i)
        squared = flat + gx * gx
        coulomb[:, i * points : (i + 1) * points] = jnp.where(
            squared > 0, (coulomb_scale / points) / jnp.maximum(squared, 1).astype(F32), 0.0
        )

    def gathered(ref, along):
        found = []
        for m in range(share):
            pieces = [
                ref[pl.ds(k * share + m if along else m * share + k, count, stride=block), :] for k in range(share)
            ]
            found.append(jnp.concatenate(pieces, 0))
        return found

    def scattered(ref, value):
        for i in range(share):
            for k in range(share):
                ref[pl.ds(i * share + k, count, stride=block), :] = value[
                    k * count : (k + 1) * count, i * points : (i + 1) * points
                ]

    drained(arrived, field_sem.at[1, 0])
    columns = jnp.concatenate(gathered(arrived, False), 1)
    scattered(slope_sent, left(lefts[5], columns))
    field_exchange(1, slope_sent, slope_got)
    scattered(wave_sent, left(lefts[4], coulomb[...] * full_dot(plain[1], columns)))
    field_exchange(2, wave_sent, wave_got)

    def to_cells(ref):
        value = left(lefts[6], jnp.concatenate(gathered(ref, True), 1))
        value = jnp.concatenate([value[:, k * points : (k + 1) * points] for k in range(share)], 0)
        return right(value, rights[:, :points])

    drained(slope_got, field_sem.at[1, 1])
    change_y = to_cells(slope_got) * (1.0 / (points * points))
    for k in range(share):
        cy = change_y[k * points : (k + 1) * points]
        gradient = jnp.sqrt(change[k] + cy * cy)
        dens = core[first_plane + k]
        for other in range(peers):
            dens = dens + parts[other, first_plane + k]
        root = jnp.exp(jnp.log(dens) * (1.0 / 3.0))
        root = root - (root * root * root - dens) / (3.0 * root * root)
        reduced = gradient / (reduced_scale * dens * root)
        bounded = reduced / (1.0 + reduced)

        def unit(h, total):
            return total + mlp_out[h] * jnp.tanh(mlp_in[0, h] * root + mlp_in[1, h] * bounded + mlp_in[2, h])

        enhance = lax.fori_loop(0, hidden, unit, jnp.ones_like(root), unroll=4)
        network[k] = external[first_plane + k] - exchange_scale * root * enhance

    drained(wave_got, field_sem.at[1, 2])
    hartree = to_cells(wave_got)

    def shared(i, seat_of, k):
        piece = out.at[seat_of * share + k]
        return remote(
            piece, piece, share_sem.at[0, i - 1, k], share_sem.at[1, i - 1, k], at(me, team + lax.rem(seat + i, sub))
        )

    for k in range(share):
        out[first_plane + k] = network[k] + hartree[k * points : (k + 1) * points]
        for i in range(1, sub):
            shared(i, seat, k).start()

    @pl.when(holder)
    def _():
        for b in range(bands):
            last(b).wait_recv()
        for b in range(bands):
            for x in range(planes):
                value = fresh[b, x] if x < slots else returned[b, x - slots]
                if x == 0:
                    clean = jnp.where(jnp.logical_and(tile_row == 0, me == home), alone, 1.0)
                    value = jnp.concatenate([value[:8] * clean, value[8:]], 0)
                swapped = pltpu.roll(value, half, 1)
                real = jnp.where(lanes < reach, value, jnp.where(lanes >= points - reach, swapped, 0.0))
                imag = jnp.where(lanes < reach, swapped, jnp.where(lanes >= points - reach, value, 0.0))
                for p, found in enumerate((real, imag)):
                    new_out[b, p, x, 0:reach] = found[:reach]
                    new_out[b, p, x, reach : reach + 8] = jnp.zeros((8, points), F32)
                    new_out[b, p, x, reach + 8 : half + 8] = found[reach:]

    @pl.when(jnp.logical_not(holder))
    def _():
        new_out[...] = jnp.zeros_like(new_out)

    @pl.when(me == 0)
    def _():
        back(0, 0).wait_recv()
        for b in range(bands):
            for p in range(2):
                z_point = lane_to(fixed_back[b], 2 + half * p, reach)
                new_out[b, p, 0, 0:8] = new_out[b, p, 0, 0:8] + z_point
                new_out[b, p, 0, reach : reach + 8] = lane_to(fixed_back[b], 3 + half * p, 0)

    @pl.when(me == zone)
    def _():
        back(0, 0).wait_recv()
        for b in range(bands):
            for p in range(2):
                new_out[b, p, 0, 0:8] = lane_to(fixed_back[b], 1 + half * p, 0)

    @pl.when(holder)
    def _():
        for b in range(bands):
            first(b).wait_send()

    @pl.when(jnp.logical_not(holder))
    def _():
        for b in range(bands):
            last(b).wait_send()

    @pl.when(me == 0)
    def _():
        fixed(0).wait_send()

    @pl.when(me == zone)
    def _():
        fixed(1).wait_send()

    @pl.when(me == home)
    def _():
        back(0, 0).wait_send()
        back(zone, 1).wait_send()

    for k in range((2 * iters + 1) * bands):
        drained(sent.at[k, pl.ds(0, n - 1)], send_sem.at[k])
    drained(gram_got.at[pl.ds(0, n - 1)], gram_sem.at[0])
    for stage, ref in enumerate((staged, slope_sent, wave_sent)):
        drained(ref.at[pl.ds(0, (count - 1) * block)], field_sem.at[0, stage])
    for i in range(1, sub):
        for k in range(share):
            shared(i, seat, k).wait_send()
            shared(i, lax.rem(seat + sub - i, sub), k).wait_recv()


def body(coefficients, potential, external, core_density, rotations, mlp_in, mlp_out):
    n, peers = lax.axis_size("grid"), lax.axis_size("band")
    bands, _, planes, points, _ = coefficients.shape
    iters = rotations.shape[0]
    half = points // 2
    slots = half // n
    sub = math.gcd(peers, planes)
    share = planes // sub
    count = n * sub
    rows = count * share * share
    stages = (2 * iters + 1) * bands
    size = (iters + 1) * bands
    tables = transform_tables(n, points, count, share)
    any_space = pl.BlockSpec(memory_space=pl.ANY)
    vmem = pl.BlockSpec(memory_space=pltpu.VMEM)
    smem = pl.BlockSpec(memory_space=pltpu.SMEM)
    dma = pltpu.SemaphoreType.DMA

    def store(*shape):
        return pltpu.VMEM(shape, F32)

    new, new_potential = pl.pallas_call(
        functools.partial(kernel, n, peers, bands, points, iters, mlp_out.shape[0]),
        out_shape=(
            jax.ShapeDtypeStruct((bands, 2, planes, half + 8, points), F32),
            jax.ShapeDtypeStruct((planes, points, points), F32),
        ),
        in_specs=[any_space] * 4 + [smem] * 3 + [vmem] * len(tables),
        out_specs=(vmem, vmem),
        scratch_shapes=[
            store(bands, 2, planes, half + 8, points),
            store(planes, points, points),
            store(planes, points, points),
            store(planes, points, points),
            store(bands, slots, half, points),
            store(bands, slots, half, points),
            store(iters + 1, bands, slots, half, points),
            store(slots, half, points),
            store(slots, half, points),
            store(stages, n, slots, planes, points),
            store(stages, n, slots, planes, points),
            store(half * planes, points),
            store(half * planes, points),
            store(16 * planes, points),
            store(16 * planes, points),
            store(size, planes, points, 2 * points),
            store(bands, 8, points),
            store(2, bands, 8, points),
            store(1, points),
            store(n, 1, points),
            store(bands, slots, half, points),
            store(bands, slots, half, points),
            store(bands, 8, points),
            store(bands, 8, points),
            store(peers, planes, points, points),
            store(points, share * points),
            store(rows, points),
            store(rows, points),
            store(rows, points),
            store(rows, points),
            store(rows, points),
            store(rows, points),
            store(share, points, points),
            store(share, points, points),
            dma((4 * bands + 3,)),
            dma((2, bands)),
            dma((3,)),
            dma((stages,)),
            dma((stages,)),
            dma((2,)),
            dma((2, bands)),
            dma((3,)),
            dma((2, max(peers - 1, 1), planes)),
            dma((2, 3)),
            dma((1,)),
            dma((2, max(sub - 1, 1), share)),
        ],
        compiler_params=pltpu.CompilerParams(
            collective_id=0, has_side_effects=True, vmem_limit_bytes=60 * 2**20
        ),
    )(coefficients, potential, external, core_density, rotations, mlp_in, mlp_out, *tables)

    reach = half // 2
    low = lax.slice_in_dim(new, 0, reach + 8, axis=3)
    high = lax.slice_in_dim(new, reach + 8, half + 8, axis=3)
    zeros = jnp.zeros((bands, 2, planes, points - half - 8, points), F32)
    return jnp.concatenate([low, zeros, high], 3), new_potential


def solution(mesh):
    in_specs = (
        P("band", None, "grid", None, None),
        P("grid", None, None),
        P("grid", None, None),
        P("grid", None, None),
        P(None, "band", None),
        P(),
        P(),
    )
    out_specs = (P("band", None, "grid", None, None), P("grid", None, None))
    return jax.shard_map(body, mesh=mesh, in_specs=in_specs, out_specs=out_specs, check_vma=False)
```

time: 179 us -> 108 us (0.60)
  the two profiles are of different devices: /device:TPU:29 before, /device:TPU:7 now
where the time goes in v1:
time: 108 us; the launch traced here: 107 us
  Pallas kernels  102 us (94%)
  local copies, waits for them, and re-layouts  3.16 us (3%)
  other arithmetic  1.64 us (2%)
    pallas_call x1, Pallas kernels, body(): pl.pallas_call(functools.partial(kernel, n, peers, bands, points, iters,...  102 us

profile of v1, /device:TPU:7, one launch (start us, length us, event | category | flops | bytes accessed | tf_op | source)
XLA Modules:
  0.0 107.4 jit_solution(17069225814139631965)
XLA Ops:
  0.6 0.1 pad.1.clone
  0.7 102.0 %shard_map.131 = (f32[2,2,8,72,128]{4,3,2,1,0:T(8,128)}, f32[8,128,128]{2,1,0:T(8,128)}) custom-call(f32[2,2,8,128,128]{4,3,2,1,0:T(8,128)} %coefficients.1, f32[8,128,128]{2,1,0:T(8,128)} %potential_in.1, f32[8,128,128]{2,1,0:T(8,128)} %external_in.1, f32[8,128,128]{2,1,0:T(8,128)} %core_in.1, f32[2,2,2]{2,1,0:T(2,128)} %rotations.1, f32[3,32]{1,0:T(4,128)} %mlp_in.1, ...), custom_call_target="tpu_custom_call" | custom-call | tf_op jit(solution)/shard_map/pallas_call | solution.py:788
  102.7 1.1 %slice.7 = f32[2,2,8,32,128]{4,3,2,1,0:T(8,128)S(1)} slice(f32[2,2,8,72,128]{4,3,2,1,0:T(8,128)} %get-tuple-element.4), slice={[0:2], [0:2], [0:8], [40:72], [0:128]} | slice | bytes 1048576 | tf_op jit(solution)/shard_map/slice | solution.py:851
  103.8 0.0 copy-start
  103.8 1.2 %slice.6 = f32[2,2,8,40,128]{4,3,2,1,0:T(8,128)S(1)} slice(f32[2,2,8,72,128]{4,3,2,1,0:T(8,128)} %get-tuple-element.4), slice={[0:2], [0:2], [0:8], [0:40], [0:128]} | slice | bytes 1310720 | tf_op jit(solution)/shard_map/slice | solution.py:850
  105.0 1.6 %pad_maximum_fusion = f32[2,2,8,128,128]{4,3,2,1,0:T(8,128)} fusion(f32[2,2,8,32,128]{4,3,2,1,0:T(8,128)S(1)} %slice.7, f32[2,2,8,40,128]{4,3,2,1,0:T(8,128)S(1)} %slice.6, f32[128]{0:T(128)S(1)} %pad.1.clone), kind=kLoop, calls=%fused_computation | loop fusion | flops 1048576 | bytes 3277312 | tf_op jit(solution)/shard_map/concatenate | solution.py:853
  106.6 0.0 copy-done
  106.6 0.8 copy.15
  (1 shorter events, 0.0 us)
Async XLA Ops:
  103.8 2.9 %copy-start = (f32[8,128,128]{2,1,0:T(8,128)S(1)}, f32[8,128,128]{2,1,0:T(8,128)}, u32[]{:S(2)}) copy-start(f32[8,128,128]{2,1,0:T(8,128)} %get-tuple-element.9) | copy-start | bytes 1572868

commit v2 on v1

--- a/solution.py
+++ b/solution.py
@@ -110,21 +110,22 @@
             derivative[order][:, order],
             basis[:, order],
             derivative,
+            basis,
         )
     ])
     rights = np.concatenate([table_for_right(basis), table_for_right(derivative.T)], 1)
     z_out = table_for_right(np.block([[cos, sin], [-sin, cos]]))
     z_in = table_for_right(np.block([[cos.T, -sin.T], [sin.T, cos.T]]))
-    plain = np.stack([basis, basis[:, order]]).astype(np.float32)
+    plain = basis[:, order][None].astype(np.float32)
     return lefts, rights, z_out, z_in, plain
 
 
 def kernel(
     n, peers, bands, points, iters, hidden,
     coefficients, potential_in, external_in, core_in, rotations, mlp_in, mlp_out,
-    lefts, rights, z_out, z_in, plain,
-    new_out, out,
-    given, potential, external, core, raw, forward, vectors, mask, kinetic,
+    lefts_in, rights_in, z_out_in, z_in_in, plain_in,
+    low_out, high_out, out,
+    tables_l, tables_r, table_out, table_in, table_plain, given, potential, external, core, raw, forward, vectors, mask, kinetic,
     sent, got, level_r, level_i, edge_r, edge_i, space_of, fixed_out, fixed_got,
     gram_tile, gram_got, fresh, returned, fixed_new, fixed_back,
     parts, coulomb, staged, arrived, slope_sent, slope_got, wave_sent, wave_got, change, network,
@@ -176,20 +177,36 @@
                 load_sem.at[k + 1],
             ))
     base = 4 * bands
+    tables = [
+        pltpu.make_async_copy(source, target, load_sem.at[base + 3 + k])
+        for k, (source, target) in enumerate((
+            (lefts_in, tables_l), (z_out_in, table_out), (z_in_in, table_in), (rights_in, tables_r), (plain_in, table_plain)
+        ))
+    ]
     late = [
         pltpu.make_async_copy(potential_in, potential, load_sem.at[base]),
         pltpu.make_async_copy(external_in, external, load_sem.at[base + 1]),
         pltpu.make_async_copy(core_in, core, load_sem.at[base + 2]),
     ]
-    for copy in loads + late:
+    needed = jnp.logical_or(holder, me == zone)
+
+    @pl.when(needed)
+    def _():
+        for copy in loads:
+            copy.start()
+
+    for copy in tables + late:
         copy.start()
 
     barrier = pltpu.get_barrier_semaphore()
 
-    @pl.loop(1, count)
+    @pl.loop(1, n)
     def _(i):
-        other = lax.rem(rank + i, count)
-        pl.semaphore_signal(barrier, inc=1, device_id=at(other // sub, team + lax.rem(other, sub)), device_id_type=MESH)
+        for k in range(sub):
+            pl.semaphore_signal(barrier, inc=1, device_id=at(lax.rem(me + i, n), team + k), device_id_type=MESH)
+
+    for k in range(1, sub):
+        pl.semaphore_signal(barrier, inc=1, device_id=at(me, team + lax.rem(seat + k, sub)), device_id_type=MESH)
 
     for i in range(1, peers):
         other = lax.rem(band + i, peers)
@@ -236,8 +253,10 @@
     edge_r[...] = jnp.zeros_like(edge_r)
     edge_i[...] = jnp.zeros_like(edge_i)
 
-    for copy in loads:
-        copy.wait()
+    @pl.when(needed)
+    def _():
+        for copy in loads:
+            copy.wait()
 
     def packed(b, x):
         found = []
@@ -282,11 +301,6 @@
     def fixed(place):
         return remote(fixed_out, fixed_got.at[place], fixed_sem.at[0], fixed_sem.at[1 + place], at(home))
 
-    @pl.when(holder)
-    def _():
-        for b in range(bands):
-            first(b).start()
-
     @pl.when(me == 0)
     def _():
         fixed(0).start()
@@ -315,13 +329,13 @@
         for x in range(slots):
             value = value_of(x)
             stacked.append(jnp.concatenate([value, turn(value)], 0))
-        full = left(lefts[0], jnp.concatenate(stacked, 1))
+        full = left(tables_l[0], jnp.concatenate(stacked, 1))
         for x in range(slots):
             sent[place, :, x] = full[:, x * points : (x + 1) * points].reshape(n, planes, points)
         exchange(place)
 
-    def space(place, action):
-        levels = right(got[place].reshape(half * planes, points), z_out[...])
+    def space(place, action, order=range(planes)):
+        levels = right(got[place].reshape(half * planes, points), table_out[...])
         level_r[...] = levels[:, :points]
         level_i[...] = levels[:, points:]
         special = got[place, home, 0]
@@ -339,10 +353,10 @@
         edge_i[pl.ds(0, planes, stride=8), :] = 2.0 * plus_i
 
         def without(value, y, extra):
-            tile = value[edge : edge + 8] - extra[y * 8 : y * 8 + 8, :]
+            tile = value[edge : edge + 8] - extra[pl.ds(pl.multiple_of(y * 8, 8), 8), :]
             return jnp.concatenate([value[:edge], tile, value[edge + 8 :]], 0)
 
-        for y in range(planes):
+        for y in order:
             real = level_r[pl.ds(y, half, stride=planes), :]
             imag = level_i[pl.ds(y, half, stride=planes), :]
             stacked = jnp.concatenate(
@@ -352,14 +366,14 @@
                 ],
                 0,
             )
-            action(y, left(lefts[2], stacked))
+            action(y, left(tables_l[2], stacked))
 
     def spectrum(index, place):
         def action(y, wave):
             space_of[index, y] = wave
             field = potential[y]
             product = wave * jnp.concatenate([field, field], 1)
-            both = left(lefts[3], product)
+            both = left(tables_l[3], product)
             cos_r, cos_i = both[:half, :points], both[:half, points:]
             sin_r, sin_i = both[half:, :points], both[half:, points:]
             level_r[pl.ds(y, half, stride=planes), :] = cos_r + sin_i
@@ -369,7 +383,7 @@
 
         space(place, action)
         both = jnp.concatenate([level_r[...], level_i[...]], 1)
-        sent[place + bands] = right(both, z_in[...]).reshape(n, slots, planes, points)
+        sent[place + bands] = right(both, table_in[...]).reshape(n, slots, planes, points)
 
         def total(value):
             return jnp.sum(value, 1, keepdims=True)
@@ -390,7 +404,7 @@
 
     def inward(place):
         columns = [got[place, :, x].reshape(points, points) for x in range(slots)]
-        both = left(lefts[1], jnp.concatenate(columns, 1))
+        both = left(tables_l[1], jnp.concatenate(columns, 1))
         found = []
         for x in range(slots):
             part = both[:, x * points : (x + 1) * points]
@@ -405,7 +419,12 @@
             v = vectors[q // bands, q % bands].reshape(slots * half, points)
             grams[q, p] = jnp.sum(u * v, 0, keepdims=True)
 
+    tables[0].wait()
     for b in range(bands):
+        @pl.when(holder)
+        def _():
+            first(b).start()
+
         @pl.when(jnp.logical_not(holder))
         def _():
             first(b).wait_recv()
@@ -427,6 +446,8 @@
         outward(lambda x: vectors[0, b, x], b)
 
     late[0].wait()
+    tables[1].wait()
+    tables[2].wait()
     size = (iters + 1) * bands
     for b in range(bands):
         measure(b)
@@ -543,14 +564,17 @@
             total = square if total is None else total + square
         parts[band, y] = total * (2.0 / (bands * peers))
         for i in range(1, peers):
-            @pl.when(lax.rem(lax.rem(band + i, peers), sub) == y // share)
+            @pl.when(lax.rem(lax.rem(band + i, peers), sub) == lax.div(y, share))
             def _():
                 density_copy(i, y).start()
 
-    space(place + bands - 1, density)
+    turns = [lax.rem(seat + 1 + m // share, sub) * share + m % share for m in range(planes)]
+    space(place + bands - 1, density, turns)
 
     late[2].wait()
     late[1].wait()
+    tables[3].wait()
+    tables[4].wait()
     for i in range(1, peers):
         for y in range(planes):
             @pl.when(lax.rem(lax.rem(band + i, peers), sub) == y // share)
@@ -570,30 +594,43 @@
         whole.append(total)
     varying = [value - level_shift for value in whole]
 
-    def field_exchange(stage, source, target):
-        def copy(other):
+    pieces = 2 if share % 2 == 0 else 1
+    piece = block // pieces
+    width = share // pieces
+
+    def field_exchange(stage, part, source, target):
+        k = stage * pieces + part
+
+        def copy(other, seat_of):
             return remote(
-                source.at[pl.ds(other * block, block)],
-                target.at[pl.ds(rank * block, block)],
-                field_sem.at[0, stage],
-                field_sem.at[1, stage],
-                at(other // sub, team + lax.rem(other, sub)),
+                source.at[pl.ds((other * sub + seat_of) * block + part * piece, piece)],
+                target.at[pl.ds(rank * block + part * piece, piece)],
+                field_sem.at[0, k],
+                field_sem.at[1, k],
+                at(other, team + seat_of),
             )
 
-        @pl.loop(1, count)
+        @pl.loop(1, n)
         def _(i):
-            copy(lax.rem(rank + i, count)).start()
-
-        pltpu.make_async_copy(
-            source.at[pl.ds(rank * block, block)], target.at[pl.ds(rank * block, block)], field_sem.at[1, stage]
-        ).start()
-
-    level = full_dot(plain[0], jnp.concatenate(varying, 1))
+            for seat_of in range(sub):
+                copy(lax.rem(me + i, n), seat_of).start()
+
+        for i in range(1, sub):
+            copy(me, lax.rem(seat + i, sub)).start()
+
+        own = pl.ds(rank * block + part * piece, piece)
+        pltpu.make_async_copy(source.at[own], target.at[own], field_sem.at[1, k]).start()
+
+    def field_drained(stage, part, ref):
+        drained(ref.at[pl.ds(0, count * piece)], field_sem.at[1, stage * pieces + part])
+
+    level = left(tables_l[8], jnp.concatenate(varying, 1))
     level = jnp.concatenate([level[:, k * points : (k + 1) * points] for k in range(share)], 0)
-    level = full_dot(level, plain[0])
+    level = right(level, tables_r[:, :points])
     for k in range(share):
         staged[pl.ds(k, points, stride=share), :] = level[k * points : (k + 1) * points]
-    field_exchange(0, staged, arrived)
+    for part in range(pieces):
+        field_exchange(0, part, staged, arrived)
 
     def last(b):
         return remote(fresh.at[b], returned.at[b], last_sem.at[0, b], last_sem.at[1, b], at(partner))
@@ -614,8 +651,8 @@
         back(zone, 1).start()
 
     columns = jnp.concatenate(varying, 1)
-    change_x = left(lefts[7], columns)
-    change_z = right(jnp.concatenate(varying, 0), rights[:, points:])
+    change_x = left(tables_l[7], columns)
+    change_z = right(jnp.concatenate(varying, 0), tables_r[:, points:])
     for k in range(share):
         cx = change_x[:, k * points : (k + 1) * points]
         cz = change_z[k * points : (k + 1) * points]
@@ -631,35 +668,37 @@
             squared > 0, (coulomb_scale / points) / jnp.maximum(squared, 1).astype(F32), 0.0
         )
 
-    def gathered(ref, along):
-        found = []
-        for m in range(share):
-            pieces = [
-                ref[pl.ds(k * share + m if along else m * share + k, count, stride=block), :] for k in range(share)
-            ]
-            found.append(jnp.concatenate(pieces, 0))
-        return found
-
-    def scattered(ref, value):
-        for i in range(share):
+    def column(ref, i):
+        return jnp.concatenate([ref[pl.ds(i * share + k, count, stride=block), :] for k in range(share)], 0)
+
+    def plane_of(ref, k):
+        return jnp.concatenate([ref[pl.ds(i * share + k, count, stride=block), :] for i in range(share)], 0)
+
+    def scattered(ref, part, value):
+        for j in range(width):
             for k in range(share):
-                ref[pl.ds(i * share + k, count, stride=block), :] = value[
-                    k * count : (k + 1) * count, i * points : (i + 1) * points
+                ref[pl.ds((part * width + j) * share + k, count, stride=block), :] = value[
+                    k * count : (k + 1) * count, j * points : (j + 1) * points
                 ]
 
-    drained(arrived, field_sem.at[1, 0])
-    columns = jnp.concatenate(gathered(arrived, False), 1)
-    scattered(slope_sent, left(lefts[5], columns))
-    field_exchange(1, slope_sent, slope_got)
-    scattered(wave_sent, left(lefts[4], coulomb[...] * full_dot(plain[1], columns)))
-    field_exchange(2, wave_sent, wave_got)
+    columns = []
+    for part in range(pieces):
+        field_drained(0, part, arrived)
+        columns.append(jnp.concatenate([column(arrived, part * width + j) for j in range(width)], 1))
+        scattered(slope_sent, part, left(tables_l[5], columns[part]))
+        field_exchange(1, part, slope_sent, slope_got)
+    for part in range(pieces):
+        weight = coulomb[:, part * width * points : (part + 1) * width * points]
+        scattered(wave_sent, part, left(tables_l[4], weight * full_dot(table_plain[0], columns[part])))
+        field_exchange(2, part, wave_sent, wave_got)
 
     def to_cells(ref):
-        value = left(lefts[6], jnp.concatenate(gathered(ref, True), 1))
+        value = left(tables_l[6], jnp.concatenate([plane_of(ref, k) for k in range(share)], 1))
         value = jnp.concatenate([value[:, k * points : (k + 1) * points] for k in range(share)], 0)
-        return right(value, rights[:, :points])
-
-    drained(slope_got, field_sem.at[1, 1])
+        return right(value, tables_r[:, :points])
+
+    for part in range(pieces):
+        field_drained(1, part, slope_got)
     change_y = to_cells(slope_got) * (1.0 / (points * points))
     for k in range(share):
         cy = change_y[k * points : (k + 1) * points]
@@ -678,20 +717,6 @@
         enhance = lax.fori_loop(0, hidden, unit, jnp.ones_like(root), unroll=4)
         network[k] = external[first_plane + k] - exchange_scale * root * enhance
 
-    drained(wave_got, field_sem.at[1, 2])
-    hartree = to_cells(wave_got)
-
-    def shared(i, seat_of, k):
-        piece = out.at[seat_of * share + k]
-        return remote(
-            piece, piece, share_sem.at[0, i - 1, k], share_sem.at[1, i - 1, k], at(me, team + lax.rem(seat + i, sub))
-        )
-
-    for k in range(share):
-        out[first_plane + k] = network[k] + hartree[k * points : (k + 1) * points]
-        for i in range(1, sub):
-            shared(i, seat, k).start()
-
     @pl.when(holder)
     def _():
         for b in range(bands):
@@ -706,13 +731,14 @@
                 real = jnp.where(lanes < reach, value, jnp.where(lanes >= points - reach, swapped, 0.0))
                 imag = jnp.where(lanes < reach, swapped, jnp.where(lanes >= points - reach, value, 0.0))
                 for p, found in enumerate((real, imag)):
-                    new_out[b, p, x, 0:reach] = found[:reach]
-                    new_out[b, p, x, reach : reach + 8] = jnp.zeros((8, points), F32)
-                    new_out[b, p, x, reach + 8 : half + 8] = found[reach:]
+                    low_out[b, p, x, 0:reach] = found[:reach]
+                    low_out[b, p, x, reach : reach + 8] = jnp.zeros((8, points), F32)
+                    high_out[b, p, x] = found[reach:]
 
     @pl.when(jnp.logical_not(holder))
     def _():
-        new_out[...] = jnp.zeros_like(new_out)
+        low_out[...] = jnp.zeros_like(low_out)
+        high_out[...] = jnp.zeros_like(high_out)
 
     @pl.when(me == 0)
     def _():
@@ -720,15 +746,30 @@
         for b in range(bands):
             for p in range(2):
                 z_point = lane_to(fixed_back[b], 2 + half * p, reach)
-                new_out[b, p, 0, 0:8] = new_out[b, p, 0, 0:8] + z_point
-                new_out[b, p, 0, reach : reach + 8] = lane_to(fixed_back[b], 3 + half * p, 0)
+                low_out[b, p, 0, 0:8] = low_out[b, p, 0, 0:8] + z_point
+                low_out[b, p, 0, reach : reach + 8] = lane_to(fixed_back[b], 3 + half * p, 0)
 
     @pl.when(me == zone)
     def _():
         back(0, 0).wait_recv()
         for b in range(bands):
             for p in range(2):
-                new_out[b, p, 0, 0:8] = lane_to(fixed_back[b], 1 + half * p, 0)
+                low_out[b, p, 0, 0:8] = lane_to(fixed_back[b], 1 + half * p, 0)
+
+    for part in range(pieces):
+        field_drained(2, part, wave_got)
+    hartree = to_cells(wave_got)
+
+    def shared(i, seat_of, k):
+        plane = out.at[seat_of * share + k]
+        return remote(
+            plane, plane, share_sem.at[0, i - 1, k], share_sem.at[1, i - 1, k], at(me, team + lax.rem(seat + i, sub))
+        )
+
+    for k in range(share):
+        out[first_plane + k] = network[k] + hartree[k * points : (k + 1) * points]
+        for i in range(1, sub):
+            shared(i, seat, k).start()
 
     @pl.when(holder)
     def _():
@@ -757,11 +798,41 @@
         drained(sent.at[k, pl.ds(0, n - 1)], send_sem.at[k])
     drained(gram_got.at[pl.ds(0, n - 1)], gram_sem.at[0])
     for stage, ref in enumerate((staged, slope_sent, wave_sent)):
-        drained(ref.at[pl.ds(0, (count - 1) * block)], field_sem.at[0, stage])
+        for part in range(pieces):
+            drained(ref.at[pl.ds(0, (count - 1) * piece)], field_sem.at[0, stage * pieces + part])
     for i in range(1, sub):
         for k in range(share):
             shared(i, seat, k).wait_send()
             shared(i, lax.rem(seat + sub - i, sub), k).wait_recv()
+
+
+def spread(bands, low, high, field, new, out, low_here, high_here, field_here, zeros, in_sem, out_sem):
+    edge, width = low.shape[3], zeros.shape[2]
+    arrivals = []
+    for b in range(bands):
+        arrivals.append(pltpu.make_async_copy(low.at[b], low_here.at[b], in_sem.at[2 * b]))
+        arrivals.append(pltpu.make_async_copy(high.at[b], high_here.at[b], in_sem.at[2 * b + 1]))
+    arrivals.append(pltpu.make_async_copy(field, field_here, in_sem.at[2 * bands]))
+    for copy in arrivals:
+        copy.start()
+    zeros[...] = jnp.zeros_like(zeros)
+    leaving = []
+    for b in range(bands):
+        leaving.append(pltpu.make_async_copy(zeros, new.at[b, :, :, pl.ds(edge, width)], out_sem.at[3 * b]))
+        leaving[-1].start()
+    for k, copy in enumerate(arrivals):
+        copy.wait()
+        b = k // 2
+        if b == bands:
+            place, source = out, field_here
+        elif k % 2 == 0:
+            place, source = new.at[b, :, :, pl.ds(0, edge)], low_here.at[b]
+        else:
+            place, source = new.at[b, :, :, pl.ds(edge + width, high.shape[3])], high_here.at[b]
+        leaving.append(pltpu.make_async_copy(source, place, out_sem.at[3 * b + 1 + k % 2 if b < bands else 3 * bands]))
+        leaving[-1].start()
+    for copy in leaving:
+        copy.wait()
 
 
 def body(coefficients, potential, external, core_density, rotations, mlp_in, mlp_out):
@@ -776,7 +847,8 @@
     rows = count * share * share
     stages = (2 * iters + 1) * bands
     size = (iters + 1) * bands
-    tables = transform_tables(n, points, count, share)
+    lefts, rights, z_out, z_in, plain = transform_tables(n, points, count, share)
+    tables = (lefts, rights, z_out, z_in, plain)
     any_space = pl.BlockSpec(memory_space=pl.ANY)
     vmem = pl.BlockSpec(memory_space=pltpu.VMEM)
     smem = pl.BlockSpec(memory_space=pltpu.SMEM)
@@ -785,15 +857,16 @@
     def store(*shape):
         return pltpu.VMEM(shape, F32)
 
-    new, new_potential = pl.pallas_call(
+    low, high, new_potential = pl.pallas_call(
         functools.partial(kernel, n, peers, bands, points, iters, mlp_out.shape[0]),
         out_shape=(
-            jax.ShapeDtypeStruct((bands, 2, planes, half + 8, points), F32),
+            jax.ShapeDtypeStruct((bands, 2, planes, half // 2 + 8, points), F32),
+            jax.ShapeDtypeStruct((bands, 2, planes, half // 2, points), F32),
             jax.ShapeDtypeStruct((planes, points, points), F32),
         ),
-        in_specs=[any_space] * 4 + [smem] * 3 + [vmem] * len(tables),
-        out_specs=(vmem, vmem),
-        scratch_shapes=[
+        in_specs=[any_space] * 4 + [smem] * 3 + [any_space] * len(tables),
+        out_specs=(vmem, vmem, vmem),
+        scratch_shapes=[pltpu.VMEM(t.shape, t.dtype) for t in tables] + [
             store(bands, 2, planes, half + 8, points),
             store(planes, points, points),
             store(planes, points, points),
@@ -828,7 +901,7 @@
             store(rows, points),
             store(share, points, points),
             store(share, points, points),
-            dma((4 * bands + 3,)),
+            dma((4 * bands + 3 + len(tables),)),
             dma((2, bands)),
             dma((3,)),
             dma((stages,)),
@@ -837,7 +910,7 @@
             dma((2, bands)),
             dma((3,)),
             dma((2, max(peers - 1, 1), planes)),
-            dma((2, 3)),
+            dma((2, 6)),
             dma((1,)),
             dma((2, max(sub - 1, 1), share)),
         ],
@@ -846,11 +919,24 @@
         ),
     )(coefficients, potential, external, core_density, rotations, mlp_in, mlp_out, *tables)
 
-    reach = half // 2
-    low = lax.slice_in_dim(new, 0, reach + 8, axis=3)
-    high = lax.slice_in_dim(new, reach + 8, half + 8, axis=3)
-    zeros = jnp.zeros((bands, 2, planes, points - half - 8, points), F32)
-    return jnp.concatenate([low, zeros, high], 3), new_potential
+    return pl.pallas_call(
+        functools.partial(spread, bands),
+        out_shape=(
+            jax.ShapeDtypeStruct((bands, 2, planes, points, points), F32),
+            jax.ShapeDtypeStruct((planes, points, points), F32),
+        ),
+        in_specs=[any_space] * 3,
+        out_specs=(any_space, any_space),
+        scratch_shapes=[
+            pltpu.VMEM(low.shape, F32),
+            pltpu.VMEM(high.shape, F32),
+            pltpu.VMEM(new_potential.shape, F32),
+            store(2, planes, points - half - 8, points),
+            dma((2 * bands + 1,)),
+            dma((3 * bands + 1,)),
+        ],
+        compiler_params=pltpu.CompilerParams(vmem_limit_bytes=60 * 2**20),
+    )(low, high, new_potential)
 
 
 def solution(mesh):

time: 108 us -> 105 us (0.972)
  local copies, waits for them, and re-layouts: 3.16 us -> 0 us
  Pallas kernels: 102 us -> 104 us
  other arithmetic: 1.64 us -> 0 us
    pallas_call x0 -> x1, Pallas kernels: none -> 2.63 us  [body(): pl.pallas_call(functools.partial(spread, bands), out_shape=(jax.ShapeDtyp...]
    slice x2 -> x0, local copies, waits for them, and re-layouts: 2.28 us -> none  [the longest x1 1.2 us: body(): low = lax.slice_in_dim(new, 0, reach + 8, axis=3)]
    concatenate x1 -> x0, other arithmetic: 1.64 us -> none  [body(): return (jnp.concatenate([low, zeros, high], 3), new_potential)]
where the time goes in v2:
time: 105 us; the launch traced here: 104 us
  Pallas kernels  104 us (99%)
    pallas_call x1, Pallas kernels, body(): pl.pallas_call(functools.partial(kernel, n, peers, bands, points, iters,...  101 us
    pallas_call x1, Pallas kernels, body(): pl.pallas_call(functools.partial(spread, bands), out_shape=(jax.ShapeDtyp...  2.63 us

profile of v2, /device:TPU:7, one launch (start us, length us, event | category | flops | bytes accessed | tf_op | source)
XLA Modules:
  0.0 104.5 jit_solution(14710401617138246934)
XLA Ops:
  0.6 101.1 %shard_map.131 = (f32[2,2,8,40,128]{4,3,2,1,0:T(8,128)}, f32[2,2,8,32,128]{4,3,2,1,0:T(8,128)}, f32[8,128,128]{2,1,0:T(8,128)}) custom-call(f32[2,2,8,128,128]{4,3,2,1,0:T(8,128)} %coefficients.1, f32[8,128,128]{2,1,0:T(8,128)} %potential_in.1, f32[8,128,128]{2,1,0:T(8,128)} %external_in.1, f32[8,128,128]{2,1,0:T(8,128)} %core_in.1, f32[2,2,2]{2,1,0:T(2,128)} %rotations.1, ...), custom_call_target="tpu_custom_call" | custom-call | tf_op jit(solution)/shard_map/pallas_call | solution.py:860
  101.7 2.6 %shard_map.132 = (f32[2,2,8,128,128]{4,3,2,1,0:T(8,128)}, f32[8,128,128]{2,1,0:T(8,128)}) custom-call(f32[2,2,8,40,128]{4,3,2,1,0:T(8,128)} %get-tuple-element.5.low, f32[2,2,8,32,128]{4,3,2,1,0:T(8,128)} %get-tuple-element.6.high, f32[8,128,128]{2,1,0:T(8,128)} %get-tuple-element.7.field), custom_call_target="tpu_custom_call" | custom-call | tf_op jit(solution)/shard_map/pallas_call | solution.py:922

commit v3 on v2

--- a/solution.py
+++ b/solution.py
@@ -65,15 +65,98 @@
     return jnp.dot(a, b, preferred_element_type=F32, precision=HIGHEST)
 
 
-def slot_planes(n, points):
-    planes, slots = points // n, points // 2 // n
-    found = []
-    for device in range(n):
-        quarter = device // (n // 4)
-        owner = device + (0, -(n // 4), n // 4, 0)[quarter]
-        start = owner * planes + (0, slots, slots, 0)[quarter]
-        found += [start + i for i in range(slots)]
-    return np.array(found)
+class Plan:
+    def __init__(self, n, points):
+        planes, slots, reach, zone = points // n, points // 2 // n, points // 4, n // 4
+        self.points, self.reach, self.planes, self.slots = points, reach, planes, slots
+        kept = list(range(reach)) + list(range(points - reach, points))
+        edge = points - reach
+        holders = list(range(zone)) + list(range(n - zone, n))
+        pairs = self.pairs(kept, edge) if slots > 1 else {}
+        owned = self.shared_rows(n, pairs, kept, holders) if len(pairs) == n // 2 else None
+        if owned is None:
+            owned = [None] * n
+            for h in holders:
+                other = h + zone if h < zone else h - zone
+                owned[h] = [(h * planes + i, None) for i in range(slots)]
+                owned[other] = [(h * planes + slots + i, None) for i in range(slots)]
+        self.owned = owned
+        self.base = min(len(rows) for rows in owned)
+        self.extra = [d for d in range(n) if len(owned[d]) > self.base]
+        if len(self.extra) == n:
+            self.base, self.extra = slots, []
+        spare = [d * slots + i for d in range(n) for i in range(len(owned[d]), slots)]
+        self.mixed, self.order, self.sends = [], [0] * (n * slots), {h: [] for h in holders}
+        self.narrow = set()
+        for d in range(n):
+            for i, (wide, narrow) in enumerate(owned[d]):
+                place = d * slots + i
+                self.order[place] = wide
+                self.sends[wide // planes].append((wide % planes, d, i, 0))
+                if narrow is not None:
+                    self.narrow.add(narrow)
+                    self.sends[narrow // planes].append((narrow % planes, d, i, 1))
+                    self.mixed.append((place, spare[len(self.mixed)], wide))
+                    self.order[self.mixed[-1][1]] = narrow
+                if edge in (wide, narrow):
+                    self.home, self.home_slot, self.home_part = d, i, 0 if edge == wide else 1
+        self.edge, self.zero = self.order.index(edge), self.order.index(0)
+
+    def freq(self, plane):
+        return plane if 2 * plane < self.points else plane - self.points
+
+    def width(self, plane):
+        return math.isqrt(self.reach**2 - self.freq(plane) ** 2)
+
+    def pairs(self, kept, edge):
+        found, used = {}, {edge}
+        for side in (1, -1):
+            group = [p for p in kept if (self.freq(p) >= 0) == (side > 0) and p != edge]
+            for narrow in sorted(group, key=self.width):
+                if narrow in used or 2 * self.width(narrow) >= self.reach - 1:
+                    continue
+                limit = self.reach - 1 - self.width(narrow)
+                fits = [p for p in group if p not in used and p != narrow and self.width(p) <= limit]
+                fits = [p for p in fits if self.width(p) > self.width(narrow)]
+                if fits:
+                    wide = max(fits, key=lambda p: (self.width(p), abs(self.freq(p))))
+                    found[wide] = narrow
+                    used |= {wide, narrow}
+        for wide in sorted(kept, reverse=True):
+            mirror = (self.points - wide) % self.points
+            if wide not in used and mirror not in used and wide > mirror and mirror in kept:
+                if 2 * self.width(wide) < self.reach:
+                    found[wide] = mirror
+                    used |= {wide, mirror}
+        close = [p for p in kept if p not in used and p // self.planes == edge // self.planes]
+        close = [p for p in close if self.width(p) <= self.reach - 4]
+        if close:
+            found[max(close, key=self.width)] = edge
+        return found
+
+    def shared_rows(self, n, pairs, kept, holders):
+        zone, slots, planes = n // 4, self.slots, self.planes
+        taken = set(pairs.values())
+        owned = [[] for _ in range(n)]
+        for group in (holders[:zone], holders[zone:]):
+            waiting = []
+            others = []
+            for h in group:
+                other = h + zone if h < zone else h - zone
+                others.append(other)
+                rows = [(p, pairs.get(p)) for p in range(h * planes, (h + 1) * planes) if p not in taken]
+                rows.sort(key=lambda row: row[1] is None)
+                owned[h] = rows[:slots]
+                owned[other] = rows[slots : 2 * slots - 1]
+                waiting += rows[2 * slots - 1 :]
+                if len(owned[h]) < slots:
+                    return None
+            for other in others:
+                while len(owned[other]) < slots - 1 and waiting:
+                    owned[other].append(waiting.pop(0))
+            if waiting or any(len(owned[other]) != slots - 1 for other in others):
+                return None
+        return owned
 
 
 def cell_order(count, share):
@@ -91,7 +174,7 @@
         return np.cos(angle), np.sin(angle)
 
     cos, sin = waves(keep)
-    plane = slot_planes(n, points)
+    plane = np.array(Plan(n, points).order)
     cos_x, sin_x = waves(np.where(2 * plane < points, plane, plane - points))
     freq = np.where(2 * cell < points, cell, cell - points)
     slope = gradient_scale * np.where(2 * freq == -points, 0, freq) / points
@@ -122,14 +205,15 @@
 
 def kernel(
     n, peers, bands, points, iters, hidden,
-    coefficients, potential_in, external_in, core_in, rotations, mlp_in, mlp_out,
+    coefficients, potential_in, external_in, core_in, rotations_in, mlp_first_in, mlp_second_in,
     lefts_in, rights_in, z_out_in, z_in_in, plain_in,
     low_out, high_out, out,
+    low_here, high_here, rotations, mlp_in, mlp_out,
     tables_l, tables_r, table_out, table_in, table_plain, given, potential, external, core, raw, forward, vectors, mask, kinetic,
     sent, got, level_r, level_i, edge_r, edge_i, space_of, fixed_out, fixed_got,
     gram_tile, gram_got, fresh, returned, fixed_new, fixed_back,
     parts, coulomb, staged, arrived, slope_sent, slope_got, wave_sent, wave_got, change, network,
-    load_sem, first_sem, fixed_sem, send_sem, recv_sem, gram_sem, last_sem, back_sem, dens_sem, field_sem, own_sem,
+    load_sem, first_send, first_recv, fixed_sem, send_sem, recv_sem, gram_sem, last_send, last_recv, back_sem, dens_sem, field_sem, out_sem,
     share_sem,
 ):
     me = lax.axis_index("grid")
@@ -139,8 +223,11 @@
     slots = half // n
     planes = points // n
     zone = n // 4
-    home = n - zone
-    edge = home * slots
+    plan = Plan(n, points)
+    base_rows, extra = plan.base, plan.extra
+    home, edge = plan.home, plan.edge
+    edge_tile, edge_row = edge // 8 * 8, edge % 8
+    zero = plan.zero * planes
     sub = math.gcd(peers, planes)
     share = planes // sub
     count = n * sub
@@ -148,10 +235,20 @@
     seat = lax.rem(band, sub)
     team = band - seat
     rank = me * sub + seat
-    holder = jnp.logical_or(me < zone, me >= home)
-    partner = jnp.where(
-        me < zone, me + zone, jnp.where(me < 2 * zone, me - zone, jnp.where(me < home, me + zone, me - zone))
-    )
+    holder = jnp.logical_or(me < zone, me >= n - zone)
+
+    def one_of(devices):
+        found = me == -1
+        for d in devices:
+            found = jnp.logical_or(found, me == d)
+        return found
+
+    def pick(values):
+        found = jnp.int32(values[0])
+        for d in range(1, n):
+            if values[d] != values[0]:
+                found = jnp.where(me == d, values[d], found)
+        return found
 
     def at(grid, other=None):
         return {"band": band if other is None else other, "grid": grid}
@@ -163,6 +260,23 @@
 
     def drained(ref, sem):
         pltpu.make_async_copy(ref, ref, sem).wait()
+
+    barrier = pltpu.get_barrier_semaphore()
+
+    @pl.loop(1, n)
+    def _(i):
+        for k in range(sub):
+            pl.semaphore_signal(barrier, inc=1, device_id=at(lax.rem(me + i, n), team + k), device_id_type=MESH)
+
+    for k in range(1, sub):
+        pl.semaphore_signal(barrier, inc=1, device_id=at(me, team + lax.rem(seat + k, sub)), device_id_type=MESH)
+
+    for i in range(1, peers):
+        other = lax.rem(band + i, peers)
+
+        @pl.when(other - lax.rem(other, sub) != team)
+        def _():
+            pl.semaphore_signal(barrier, inc=1, device_id=at(me, other), device_id_type=MESH)
 
     loads = []
     for b in range(bands):
@@ -187,6 +301,9 @@
         pltpu.make_async_copy(potential_in, potential, load_sem.at[base]),
         pltpu.make_async_copy(external_in, external, load_sem.at[base + 1]),
         pltpu.make_async_copy(core_in, core, load_sem.at[base + 2]),
+        pltpu.make_async_copy(rotations_in, rotations, load_sem.at[base + 3 + len(tables)]),
+        pltpu.make_async_copy(mlp_first_in, mlp_in, load_sem.at[base + 4 + len(tables)]),
+        pltpu.make_async_copy(mlp_second_in, mlp_out, load_sem.at[base + 5 + len(tables)]),
     ]
     needed = jnp.logical_or(holder, me == zone)
 
@@ -197,23 +314,6 @@
 
     for copy in tables + late:
         copy.start()
-
-    barrier = pltpu.get_barrier_semaphore()
-
-    @pl.loop(1, n)
-    def _(i):
-        for k in range(sub):
-            pl.semaphore_signal(barrier, inc=1, device_id=at(lax.rem(me + i, n), team + k), device_id_type=MESH)
-
-    for k in range(1, sub):
-        pl.semaphore_signal(barrier, inc=1, device_id=at(me, team + lax.rem(seat + k, sub)), device_id_type=MESH)
-
-    for i in range(1, peers):
-        other = lax.rem(band + i, peers)
-
-        @pl.when(other - lax.rem(other, sub) != team)
-        def _():
-            pl.semaphore_signal(barrier, inc=1, device_id=at(me, other), device_id_type=MESH)
 
     lanes = lax.broadcasted_iota(jnp.int32, (1, points), 1)
     tile_lane = lax.broadcasted_iota(jnp.int32, (8, points), 1)
@@ -236,18 +336,30 @@
     def frequency(place):
         return jnp.where(2 * place < points, place, place - points)
 
-    own_start = jnp.where(holder, me * planes, partner * planes + slots)
     row = lax.broadcasted_iota(jnp.int32, (half, points), 0)
     gy = jnp.where(row < reach, row, row - half)
-    lane = lax.rem(lax.broadcasted_iota(jnp.int32, (half, points), 1), half)
-    gz = jnp.where(lane < reach, lane, lane - half)
-    flat = gy * gy + gz * gz
+    lane = lax.rem(lanes, half)
+    lane_far = lax.rem(lane + reach, half)
+
+    def centred(value):
+        return jnp.where(value < reach, value, value - half)
+
+    def swap(value):
+        return jnp.where(lane < reach, pltpu.roll(value, points - reach, 1), pltpu.roll(value, reach, 1))
+
+    gz, gz_far = centred(lane), centred(lane_far)
+    flat, flat_far = gy * gy + gz * gz, gy * gy + gz_far * gz_far
+    outer = []
     for x in range(slots):
-        gx = frequency(own_start + x)
-        squared = flat + gx * gx
-        if x == 0:
-            spot = jnp.logical_and(jnp.logical_and(row == 0, lane < 4), me == home)
-            squared = jnp.where(spot, reach * reach, squared)
+        rows = [plan.owned[d][x] if x < len(plan.owned[d]) else (None, None) for d in range(n)]
+        gx = pick([points if wide is None else plan.freq(wide) for wide, _ in rows])
+        gx_far = pick([points if narrow is None else plan.freq(narrow) for _, narrow in rows])
+        outer.append(gx * gx + gz * gz > reach * reach)
+        squared = jnp.where(outer[x], flat_far + gx_far * gx_far, flat + gx * gx)
+        if x == plan.home_slot:
+            spot = jnp.logical_and(row == 0, me == home)
+            where = jnp.logical_and(outer[x], lane_far < 4) if plan.home_part else lane < 4
+            squared = jnp.where(jnp.logical_and(spot, where), reach * reach, squared)
         mask[x] = jnp.where(16 * squared <= points * points, 1.0, 0.0).astype(F32)
         kinetic[x] = kinetic_scale * squared.astype(F32) / (points * points)
     edge_r[...] = jnp.zeros_like(edge_r)
@@ -270,9 +382,14 @@
     @pl.when(holder)
     def _():
         for b in range(bands):
-            for x in range(slots):
-                forward[b, x] = packed(b, slots + x)
-                raw[b, x] = packed(b, x)
+            for x in range(planes):
+                forward[b, x] = packed(b, x)
+
+    if extra:
+        @pl.when(jnp.logical_not(one_of(extra)))
+        def _():
+            for b in range(bands):
+                raw[0, b, base_rows] = jnp.zeros((half, points), F32)
 
     def lane_to(value, start, target):
         moved = pltpu.roll(value, (target - start) % points, 1)
@@ -295,8 +412,40 @@
 
     pl.semaphore_wait(barrier, count - 1 + peers - sub)
 
-    def first(b):
-        return remote(forward.at[b], raw.at[b], first_sem.at[0, b], first_sem.at[1, b], at(partner))
+    def first(b, h, entry):
+        x, d, i, part = entry
+        target, sem = raw.at[part, b, i], first_recv.at[part, b, i]
+        if d == h:
+            return pltpu.make_async_copy(forward.at[b, x], target, sem)
+        return remote(forward.at[b, x], target, first_send.at[b, x], sem, at(d))
+
+    def distribute(b):
+        for h, entries in plan.sends.items():
+            @pl.when(me == h)
+            def _():
+                for entry in sorted(entries, key=lambda e: e[1] == h):
+                    first(b, h, entry).start()
+
+    def gather(b):
+        for x in range(slots):
+            for part in range(2):
+                devices = [
+                    d for d in range(n) if x < len(plan.owned[d]) and plan.owned[d][x][part] is not None
+                ]
+                if len(devices) == n:
+                    drained(raw.at[part, b, x], first_recv.at[part, b, x])
+                elif devices:
+                    @pl.when(one_of(devices))
+                    def _():
+                        drained(raw.at[part, b, x], first_recv.at[part, b, x])
+
+    def merge(b):
+        for x in range(slots):
+            devices = [d for d in range(n) if x < len(plan.owned[d]) and plan.owned[d][x][1] is not None]
+            if devices:
+                @pl.when(one_of(devices))
+                def _():
+                    raw[0, b, x] = jnp.where(outer[x], swap(raw[1, b, x]), raw[0, b, x])
 
     def fixed(place):
         return remote(fixed_out, fixed_got.at[place], fixed_sem.at[0], fixed_sem.at[1 + place], at(home))
@@ -309,20 +458,62 @@
     def _():
         fixed(1).start()
 
-    def exchange(place):
-        def copy(target):
-            return remote(
-                sent.at[place, target], got.at[place, me], send_sem.at[place], recv_sem.at[place], at(target)
-            )
-
+    def part_copy(place, target, part):
+        rows = pl.ds(0, base_rows) if part == 0 else pl.ds(base_rows, 1)
+        return remote(
+            sent.at[place, target, rows], got.at[place, me, rows],
+            send_sem.at[part, place], recv_sem.at[part, place], at(target),
+        )
+
+    def own_copy(place, part):
+        rows = pl.ds(0, base_rows) if part == 0 else pl.ds(base_rows, 1)
+        return pltpu.make_async_copy(sent.at[place, me, rows], got.at[place, me, rows], recv_sem.at[part, place])
+
+    def is_extra(device):
+        return jnp.logical_or(device < zone, device >= n - zone)
+
+    if extra:
+        assert extra == list(range(zone)) + list(range(n - zone, n))
+
+    def exchange(place, to_cells):
         @pl.loop(1, n)
         def _(i):
-            copy(lax.rem(me + i, n)).start()
-
-        pltpu.make_async_copy(sent.at[place, me], got.at[place, me], recv_sem.at[place]).start()
-
-    def received(place):
-        drained(got.at[place], recv_sem.at[place])
+            target = lax.rem(me + i, n)
+            part_copy(place, target, 0).start()
+            if extra:
+                @pl.when(is_extra(me if to_cells else target))
+                def _():
+                    part_copy(place, target, 1).start()
+
+        own_copy(place, 0).start()
+        if extra:
+            @pl.when(is_extra(me))
+            def _():
+                own_copy(place, 1).start()
+
+    def received(place, to_cells):
+        drained(got.at[place, pl.ds(0, n), pl.ds(0, base_rows)], recv_sem.at[0, place])
+        if extra and to_cells:
+            drained(got.at[place, pl.ds(0, len(extra)), base_rows], recv_sem.at[1, place])
+        elif extra:
+            @pl.when(is_extra(me))
+            def _():
+                drained(got.at[place, pl.ds(0, n), base_rows], recv_sem.at[1, place])
+
+    def all_sent(place, to_cells):
+        drained(sent.at[place, pl.ds(0, n - 1), pl.ds(0, base_rows)], send_sem.at[0, place])
+        if extra and to_cells:
+            @pl.when(is_extra(me))
+            def _():
+                drained(sent.at[place, pl.ds(0, n - 1), base_rows], send_sem.at[1, place])
+        elif extra:
+            @pl.when(is_extra(me))
+            def _():
+                drained(sent.at[place, pl.ds(0, len(extra) - 1), base_rows], send_sem.at[1, place])
+
+            @pl.when(jnp.logical_not(is_extra(me)))
+            def _():
+                drained(sent.at[place, pl.ds(0, len(extra)), base_rows], send_sem.at[1, place])
 
     def outward(value_of, place):
         stacked = []
@@ -332,13 +523,18 @@
         full = left(tables_l[0], jnp.concatenate(stacked, 1))
         for x in range(slots):
             sent[place, :, x] = full[:, x * points : (x + 1) * points].reshape(n, planes, points)
-        exchange(place)
+        exchange(place, True)
 
     def space(place, action, order=range(planes)):
+        for wide, narrow, plane in plan.mixed:
+            value = got[place, wide // slots, wide % slots]
+            far = gz * gz + plan.freq(plane) ** 2 > reach * reach
+            got[place, narrow // slots, narrow % slots] = swap(jnp.where(far, value, 0.0))
+            got[place, wide // slots, wide % slots] = jnp.where(far, 0.0, value)
         levels = right(got[place].reshape(half * planes, points), table_out[...])
         level_r[...] = levels[:, :points]
         level_i[...] = levels[:, points:]
-        special = got[place, home, 0]
+        special = got[place, edge // slots, edge % slots]
 
         def lane_of(k):
             return jnp.broadcast_to(special[:, k : k + 1], (planes, points))
@@ -347,14 +543,14 @@
         minus_i, plus_i, z_i, y_i = [lane_of(half + k) for k in range(4)]
         level_r[edge * planes : (edge + 1) * planes, :] = minus_r + plus_r
         level_i[edge * planes : (edge + 1) * planes, :] = minus_i + plus_i
-        level_r[0:planes, :] += z_r * z_c - z_i * z_s + y_r * y_c - y_i * y_s
-        level_i[0:planes, :] += z_r * z_s + z_i * z_c + y_r * y_s + y_i * y_c
-        edge_r[pl.ds(0, planes, stride=8), :] = 2.0 * plus_r
-        edge_i[pl.ds(0, planes, stride=8), :] = 2.0 * plus_i
+        level_r[zero : zero + planes, :] += z_r * z_c - z_i * z_s + y_r * y_c - y_i * y_s
+        level_i[zero : zero + planes, :] += z_r * z_s + z_i * z_c + y_r * y_s + y_i * y_c
+        edge_r[pl.ds(edge_row, planes, stride=8), :] = 2.0 * plus_r
+        edge_i[pl.ds(edge_row, planes, stride=8), :] = 2.0 * plus_i
 
         def without(value, y, extra):
-            tile = value[edge : edge + 8] - extra[pl.ds(pl.multiple_of(y * 8, 8), 8), :]
-            return jnp.concatenate([value[:edge], tile, value[edge + 8 :]], 0)
+            tile = value[edge_tile : edge_tile + 8] - extra[pl.ds(pl.multiple_of(y * 8, 8), 8), :]
+            return jnp.concatenate([value[:edge_tile], tile, value[edge_tile + 8 :]], 0)
 
         for y in order:
             real = level_r[pl.ds(y, half, stride=planes), :]
@@ -378,8 +574,8 @@
             sin_r, sin_i = both[half:, :points], both[half:, points:]
             level_r[pl.ds(y, half, stride=planes), :] = cos_r + sin_i
             level_i[pl.ds(y, half, stride=planes), :] = cos_i - sin_r
-            edge_r[8 * (planes + y) : 8 * (planes + y) + 8, :] = cos_r[edge : edge + 8] - sin_i[edge : edge + 8]
-            edge_i[8 * (planes + y) : 8 * (planes + y) + 8, :] = cos_i[edge : edge + 8] + sin_r[edge : edge + 8]
+            edge_r[8 * (planes + y) : 8 * (planes + y) + 8, :] = cos_r[edge_tile : edge_tile + 8] - sin_i[edge_tile : edge_tile + 8]
+            edge_i[8 * (planes + y) : 8 * (planes + y) + 8, :] = cos_i[edge_tile : edge_tile + 8] + sin_r[edge_tile : edge_tile + 8]
 
         space(place, action)
         both = jnp.concatenate([level_r[...], level_i[...]], 1)
@@ -388,19 +584,24 @@
         def total(value):
             return jnp.sum(value, 1, keepdims=True)
 
-        plus_r = edge_r[pl.ds(8 * planes, planes, stride=8), :]
-        plus_i = edge_i[pl.ds(8 * planes, planes, stride=8), :]
-        zero_r, zero_i = level_r[0:planes, :], level_i[0:planes, :]
+        plus_r = edge_r[pl.ds(8 * planes + edge_row, planes, stride=8), :]
+        plus_i = edge_i[pl.ds(8 * planes + edge_row, planes, stride=8), :]
+        zero_r, zero_i = level_r[zero : zero + planes, :], level_i[zero : zero + planes, :]
         line_r, line_i = total(zero_r), total(zero_i)
         found = [
             total(plus_r), total(zero_r * z_c + zero_i * z_s), line_r * y_c + line_i * y_s,
             total(plus_i), total(zero_i * z_c - zero_r * z_s), line_i * y_c - line_r * y_s,
         ]
-        special = sent[place + bands, home, 0] * alone
+        special = sent[place + bands, edge // slots, edge % slots] * alone
         for k, value in enumerate(found):
             special = jnp.where(lanes == (k + 1 if k < 3 else half + k - 2), value, special)
-        sent[place + bands, home, 0] = special
-        exchange(place + bands)
+        sent[place + bands, edge // slots, edge % slots] = special
+        for wide, narrow, plane in plan.mixed:
+            far = gz * gz + plan.freq(plane) ** 2 > reach * reach
+            value = sent[place + bands, narrow // slots, narrow % slots]
+            kept = sent[place + bands, wide // slots, wide % slots]
+            sent[place + bands, wide // slots, wide % slots] = jnp.where(far, swap(value), kept)
+        exchange(place + bands, False)
 
     def inward(place):
         columns = [got[place, :, x].reshape(points, points) for x in range(slots)]
@@ -421,14 +622,8 @@
 
     tables[0].wait()
     for b in range(bands):
-        @pl.when(holder)
-        def _():
-            first(b).start()
-
-        @pl.when(jnp.logical_not(holder))
-        def _():
-            first(b).wait_recv()
-
+        distribute(b)
+        gather(b)
         if b == 0:
             @pl.when(me == home)
             def _():
@@ -440,12 +635,15 @@
         @pl.when(me == home)
         def _():
             clean = jnp.where(tile_row == 0, alone, 1.0)
-            raw[b, 0, 0:8, :] = raw[b, 0, 0:8, :] * clean * mask[0, 0:8, :] + fixed_got[0, b]
-
-        vectors[0, b] = raw[b] * mask[...]
+            tile = raw[plan.home_part, b, plan.home_slot, 0:8, :]
+            raw[plan.home_part, b, plan.home_slot, 0:8, :] = tile * clean + fixed_got[0, b]
+
+        merge(b)
+        vectors[0, b] = jnp.where(mask[...] > 0.0, raw[0, b], 0.0)
         outward(lambda x: vectors[0, b, x], b)
 
     late[0].wait()
+    late[3].wait()
     tables[1].wait()
     tables[2].wait()
     size = (iters + 1) * bands
@@ -453,16 +651,15 @@
         measure(b)
     for t in range(iters):
         for b in range(bands):
-            received(2 * t * bands + b)
+            received(2 * t * bands + b, True)
             spectrum(t * bands + b, 2 * t * bands + b)
         for b in range(bands):
             place = (2 * t + 1) * bands + b
-            received(place)
+            received(place, False)
             found = inward(place)
             for x in range(slots):
-                vectors[t + 1, b, x] = mask[x] * (
-                    kinetic[x] * vectors[t, b, x] + found[x] * (1.0 / points**3)
-                )
+                value = kinetic[x] * vectors[t, b, x] + found[x] * (1.0 / points**3)
+                vectors[t + 1, b, x] = jnp.where(mask[x] > 0.0, value, 0.0)
             last = (t + 1) * bands + b == size - 1
             if last:
                 measure(size - 1)
@@ -533,7 +730,7 @@
 
     place = 2 * iters * bands
     for b in range(bands - 1):
-        received(place + b)
+        received(place + b, True)
 
         def keep(y, wave):
             space_of[iters * bands + b, y] = wave
@@ -553,7 +750,7 @@
             parts.at[band, y], parts.at[band, y], dens_sem.at[0, i - 1, y], dens_sem.at[1, i - 1, y], at(me, target)
         )
 
-    received(place + bands - 1)
+    received(place + bands - 1, True)
 
     def density(y, wave):
         total = None
@@ -573,6 +770,8 @@
 
     late[2].wait()
     late[1].wait()
+    late[4].wait()
+    late[5].wait()
     tables[3].wait()
     tables[4].wait()
     for i in range(1, peers):
@@ -632,21 +831,36 @@
     for part in range(pieces):
         field_exchange(0, part, staged, arrived)
 
-    def last(b):
-        return remote(fresh.at[b], returned.at[b], last_sem.at[0, b], last_sem.at[1, b], at(partner))
+    def returning(b, d, remote_only=False):
+        found = []
+        for i, planes_of in enumerate(plan.owned[d]):
+            for part, plane in enumerate(planes_of):
+                if plane is None:
+                    continue
+                h, x = plane // planes, plane % planes
+                if h != d:
+                    found.append(remote(
+                        fresh.at[b, i], returned.at[b, x], last_send.at[b, i, part], last_recv.at[b, x], at(h)
+                    ))
+                elif not remote_only:
+                    found.append(pltpu.make_async_copy(fresh.at[b, i], returned.at[b, x], last_recv.at[b, x]))
+        return found
 
     def back(target, sem):
         return remote(fixed_new, fixed_back, back_sem.at[sem], back_sem.at[2], at(target))
 
-    @pl.when(jnp.logical_not(holder))
-    def _():
-        for b in range(bands):
-            last(b).start()
+    for d in range(n):
+        @pl.when(me == d)
+        def _():
+            for b in range(bands):
+                for copy in returning(b, d):
+                    copy.start()
 
     @pl.when(me == home)
     def _():
         for b in range(bands):
-            fixed_new[b] = fresh[b, 0, 0:8, :]
+            tile = fresh[b, plan.home_slot, 0:8, :]
+            fixed_new[b] = swap(tile) if plan.home_part else tile
         back(0, 0).start()
         back(zone, 1).start()
 
@@ -657,13 +871,12 @@
         cx = change_x[:, k * points : (k + 1) * points]
         cz = change_z[k * points : (k + 1) * points]
         change[k] = cx * cx + cz * cz
-    row = lax.broadcasted_iota(jnp.int32, (points, points), 0)
-    lane = lax.broadcasted_iota(jnp.int32, (points, points), 1)
-    gy, gz = frequency(row), frequency(lane)
-    flat = gy * gy + gz * gz
+    gy_all = frequency(lax.broadcasted_iota(jnp.int32, (points, points), 0))
+    gz_all = frequency(lax.broadcasted_iota(jnp.int32, (points, points), 1))
+    flat_all = gy_all * gy_all + gz_all * gz_all
     for i in range(share):
         gx = frequency(rank * share + i)
-        squared = flat + gx * gx
+        squared = flat_all + gx * gx
         coulomb[:, i * points : (i + 1) * points] = jnp.where(
             squared > 0, (coulomb_scale / points) / jnp.maximum(squared, 1).astype(F32), 0.0
         )
@@ -696,6 +909,54 @@
         value = left(tables_l[6], jnp.concatenate([plane_of(ref, k) for k in range(share)], 1))
         value = jnp.concatenate([value[:, k * points : (k + 1) * points] for k in range(share)], 0)
         return right(value, tables_r[:, :points])
+
+    @pl.when(holder)
+    def _():
+        for x in range(planes):
+            narrow = [p // planes for p in sorted(plan.narrow) if p % planes == x]
+            gx = frequency(me * planes + x)
+            inside = 16 * (flat + gx * gx) <= points * points
+            for b in range(bands):
+                drained(returned.at[b, x], last_recv.at[b, x])
+                value = returned[b, x]
+                if narrow:
+                    value = jnp.where(one_of(narrow), swap(value), value)
+                value = jnp.where(inside, value, 0.0)
+                swapped = pltpu.roll(value, half, 1)
+                real = jnp.where(lanes < reach, value, jnp.where(lanes >= points - reach, swapped, 0.0))
+                imag = jnp.where(lanes < reach, swapped, jnp.where(lanes >= points - reach, value, 0.0))
+                for p, found in enumerate((real, imag)):
+                    low_here[b, p, x, 0:reach] = found[:reach]
+                    low_here[b, p, x, reach : reach + 8] = jnp.zeros((8, points), F32)
+                    high_here[b, p, x] = found[reach:]
+
+    @pl.when(jnp.logical_not(holder))
+    def _():
+        low_here[...] = jnp.zeros_like(low_here)
+        high_here[...] = jnp.zeros_like(high_here)
+
+    @pl.when(me == 0)
+    def _():
+        back(0, 0).wait_recv()
+        for b in range(bands):
+            for p in range(2):
+                z_point = lane_to(fixed_back[b], 2 + half * p, reach)
+                low_here[b, p, 0, 0:8] = low_here[b, p, 0, 0:8] + z_point
+                low_here[b, p, 0, reach : reach + 8] = lane_to(fixed_back[b], 3 + half * p, 0)
+
+    @pl.when(me == zone)
+    def _():
+        back(0, 0).wait_recv()
+        for b in range(bands):
+            for p in range(2):
+                low_here[b, p, 0, 0:8] = lane_to(fixed_back[b], 1 + half * p, 0)
+
+    leaving = [
+        pltpu.make_async_copy(low_here, low_out, out_sem.at[0]),
+        pltpu.make_async_copy(high_here, high_out, out_sem.at[1]),
+    ]
+    for copy in leaving:
+        copy.start()
 
     for part in range(pieces):
         field_drained(1, part, slope_got)
@@ -711,75 +972,48 @@
         reduced = gradient / (reduced_scale * dens * root)
         bounded = reduced / (1.0 + reduced)
 
-        def unit(h, total):
-            return total + mlp_out[h] * jnp.tanh(mlp_in[0, h] * root + mlp_in[1, h] * bounded + mlp_in[2, h])
-
-        enhance = lax.fori_loop(0, hidden, unit, jnp.ones_like(root), unroll=4)
-        network[k] = external[first_plane + k] - exchange_scale * root * enhance
-
-    @pl.when(holder)
-    def _():
-        for b in range(bands):
-            last(b).wait_recv()
-        for b in range(bands):
-            for x in range(planes):
-                value = fresh[b, x] if x < slots else returned[b, x - slots]
-                if x == 0:
-                    clean = jnp.where(jnp.logical_and(tile_row == 0, me == home), alone, 1.0)
-                    value = jnp.concatenate([value[:8] * clean, value[8:]], 0)
-                swapped = pltpu.roll(value, half, 1)
-                real = jnp.where(lanes < reach, value, jnp.where(lanes >= points - reach, swapped, 0.0))
-                imag = jnp.where(lanes < reach, swapped, jnp.where(lanes >= points - reach, value, 0.0))
-                for p, found in enumerate((real, imag)):
-                    low_out[b, p, x, 0:reach] = found[:reach]
-                    low_out[b, p, x, reach : reach + 8] = jnp.zeros((8, points), F32)
-                    high_out[b, p, x] = found[reach:]
-
-    @pl.when(jnp.logical_not(holder))
-    def _():
-        low_out[...] = jnp.zeros_like(low_out)
-        high_out[...] = jnp.zeros_like(high_out)
-
-    @pl.when(me == 0)
-    def _():
-        back(0, 0).wait_recv()
-        for b in range(bands):
-            for p in range(2):
-                z_point = lane_to(fixed_back[b], 2 + half * p, reach)
-                low_out[b, p, 0, 0:8] = low_out[b, p, 0, 0:8] + z_point
-                low_out[b, p, 0, reach : reach + 8] = lane_to(fixed_back[b], 3 + half * p, 0)
-
-    @pl.when(me == zone)
-    def _():
-        back(0, 0).wait_recv()
-        for b in range(bands):
-            for p in range(2):
-                low_out[b, p, 0, 0:8] = lane_to(fixed_back[b], 1 + half * p, 0)
+        for first_row in range(0, points, points // 2):
+            r = root[first_row : first_row + points // 2]
+            q = bounded[first_row : first_row + points // 2]
+
+            def unit(h, total):
+                return total + mlp_out[h] * jnp.tanh(mlp_in[0, h] * r + mlp_in[1, h] * q + mlp_in[2, h])
+
+            enhance = lax.fori_loop(0, hidden, unit, jnp.ones_like(r), unroll=8)
+            rows = pl.ds(first_row, points // 2)
+            network[k, rows] = external[first_plane + k, rows] - exchange_scale * r * enhance
 
     for part in range(pieces):
         field_drained(2, part, wave_got)
     hartree = to_cells(wave_got)
 
     def shared(i, seat_of, k):
-        plane = out.at[seat_of * share + k]
         return remote(
-            plane, plane, share_sem.at[0, i - 1, k], share_sem.at[1, i - 1, k], at(me, team + lax.rem(seat + i, sub))
+            network.at[k], out.at[seat_of * share + k],
+            share_sem.at[0, i - 1, k], share_sem.at[1, i - 1, k], at(me, team + lax.rem(seat + i, sub)),
         )
 
     for k in range(share):
-        out[first_plane + k] = network[k] + hartree[k * points : (k + 1) * points]
+        network[k] = network[k] + hartree[k * points : (k + 1) * points]
         for i in range(1, sub):
             shared(i, seat, k).start()
-
-    @pl.when(holder)
-    def _():
-        for b in range(bands):
-            first(b).wait_send()
-
-    @pl.when(jnp.logical_not(holder))
-    def _():
-        for b in range(bands):
-            last(b).wait_send()
+        leaving.append(pltpu.make_async_copy(network.at[k], out.at[first_plane + k], out_sem.at[2 + k]))
+        leaving[-1].start()
+
+    for h, entries in plan.sends.items():
+        @pl.when(me == h)
+        def _():
+            for b in range(bands):
+                for entry in entries:
+                    if entry[1] != h:
+                        first(b, h, entry).wait_send()
+
+    for d in range(n):
+        @pl.when(me == d)
+        def _():
+            for b in range(bands):
+                for copy in returning(b, d, True):
+                    copy.wait_send()
 
     @pl.when(me == 0)
     def _():
@@ -795,7 +1029,7 @@
         back(zone, 1).wait_send()
 
     for k in range((2 * iters + 1) * bands):
-        drained(sent.at[k, pl.ds(0, n - 1)], send_sem.at[k])
+        all_sent(k, k // bands % 2 == 0)
     drained(gram_got.at[pl.ds(0, n - 1)], gram_sem.at[0])
     for stage, ref in enumerate((staged, slope_sent, wave_sent)):
         for part in range(pieces):
@@ -804,6 +1038,8 @@
         for k in range(share):
             shared(i, seat, k).wait_send()
             shared(i, lax.rem(seat + sub - i, sub), k).wait_recv()
+    for copy in leaving:
+        copy.wait()
 
 
 def spread(bands, low, high, field, new, out, low_here, high_here, field_here, zeros, in_sem, out_sem):
@@ -850,8 +1086,6 @@
     lefts, rights, z_out, z_in, plain = transform_tables(n, points, count, share)
     tables = (lefts, rights, z_out, z_in, plain)
     any_space = pl.BlockSpec(memory_space=pl.ANY)
-    vmem = pl.BlockSpec(memory_space=pltpu.VMEM)
-    smem = pl.BlockSpec(memory_space=pltpu.SMEM)
     dma = pltpu.SemaphoreType.DMA
 
     def store(*shape):
@@ -864,15 +1098,21 @@
             jax.ShapeDtypeStruct((bands, 2, planes, half // 2, points), F32),
             jax.ShapeDtypeStruct((planes, points, points), F32),
         ),
-        in_specs=[any_space] * 4 + [smem] * 3 + [any_space] * len(tables),
-        out_specs=(vmem, vmem, vmem),
-        scratch_shapes=[pltpu.VMEM(t.shape, t.dtype) for t in tables] + [
+        in_specs=[any_space] * (7 + len(tables)),
+        out_specs=(any_space, any_space, any_space),
+        scratch_shapes=[
+            store(bands, 2, planes, half // 2 + 8, points),
+            store(bands, 2, planes, half // 2, points),
+            pltpu.SMEM(rotations.shape, F32),
+            pltpu.SMEM(mlp_in.shape, F32),
+            pltpu.SMEM(mlp_out.shape, F32),
+        ] + [pltpu.VMEM(t.shape, t.dtype) for t in tables] + [
             store(bands, 2, planes, half + 8, points),
             store(planes, points, points),
             store(planes, points, points),
             store(planes, points, points),
-            store(bands, slots, half, points),
-            store(bands, slots, half, points),
+            store(2, bands, slots, half, points),
+            store(bands, planes, half, points),
             store(iters + 1, bands, slots, half, points),
             store(slots, half, points),
             store(slots, half, points),
@@ -888,7 +1128,7 @@
             store(1, points),
             store(n, 1, points),
             store(bands, slots, half, points),
-            store(bands, slots, half, points),
+            store(bands, planes, half, points),
             store(bands, 8, points),
             store(bands, 8, points),
             store(peers, planes, points, points),
@@ -901,17 +1141,19 @@
             store(rows, points),
             store(share, points, points),
             store(share, points, points),
-            dma((4 * bands + 3 + len(tables),)),
-            dma((2, bands)),
+            dma((4 * bands + 6 + len(tables),)),
+            dma((bands, planes)),
+            dma((2, bands, slots)),
             dma((3,)),
-            dma((stages,)),
-            dma((stages,)),
+            dma((2, stages)),
+            dma((2, stages)),
             dma((2,)),
-            dma((2, bands)),
+            dma((bands, slots, 2)),
+            dma((bands, planes)),
             dma((3,)),
             dma((2, max(peers - 1, 1), planes)),
             dma((2, 6)),
-            dma((1,)),
+            dma((2 + share,)),
             dma((2, max(sub - 1, 1), share)),
         ],
         compiler_params=pltpu.CompilerParams(

time: 105 us -> 101 us (0.962); the launches traced: 104 us -> 99.3 us
  Pallas kernels: 104 us -> 98.5 us
    pallas_call x1, Pallas kernels: 101 us -> 95.9 us  [body(): pl.pallas_call(functools.partial(kernel, n, peers, bands, points, iters,...]
where the time goes in v3:
time: 101 us; the launch traced here: 99.3 us
  Pallas kernels  98.5 us (98%)
    pallas_call x1, Pallas kernels, body(): pl.pallas_call(functools.partial(kernel, n, peers, bands, points, iters,...  95.9 us
    pallas_call x1, Pallas kernels, body(): pl.pallas_call(functools.partial(spread, bands), out_shape=(jax.ShapeDtyp...  2.63 us

profile of v3, /device:TPU:7, one launch (start us, length us, event | category | flops | bytes accessed | tf_op | source)
XLA Modules:
  0.0 99.3 jit_solution(2914603827491177235)
XLA Ops:
  0.6 95.9 %shard_map.131 = (f32[2,2,8,40,128]{4,3,2,1,0:T(8,128)}, f32[2,2,8,32,128]{4,3,2,1,0:T(8,128)}, f32[8,128,128]{2,1,0:T(8,128)}) custom-call(f32[2,2,8,128,128]{4,3,2,1,0:T(8,128)} %coefficients.1, f32[8,128,128]{2,1,0:T(8,128)} %potential_in.1, f32[8,128,128]{2,1,0:T(8,128)} %external_in.1, f32[8,128,128]{2,1,0:T(8,128)} %core_in.1, ...), custom_call_target="tpu_custom_call" | custom-call | tf_op jit(solution)/shard_map/pallas_call | solution.py:1094
  96.5 2.6 %shard_map.132 = (f32[2,2,8,128,128]{4,3,2,1,0:T(8,128)}, f32[8,128,128]{2,1,0:T(8,128)}) custom-call(f32[2,2,8,40,128]{4,3,2,1,0:T(8,128)} %get-tuple-element.5.low, f32[2,2,8,32,128]{4,3,2,1,0:T(8,128)} %get-tuple-element.6.high, f32[8,128,128]{2,1,0:T(8,128)} %get-tuple-element.7.field), custom_call_target="tpu_custom_call" | custom-call | tf_op jit(solution)/shard_map/pallas_call | solution.py:1164

commit v4 on v3

--- a/solution.py
+++ b/solution.py
@@ -623,6 +623,7 @@
     tables[0].wait()
     for b in range(bands):
         distribute(b)
+    for b in range(bands):
         gather(b)
         if b == 0:
             @pl.when(me == home)

time: 101 us -> 97.2 us (0.962)
  Pallas kernels: 98.5 us -> 95.7 us
    pallas_call x1, Pallas kernels: 95.9 us -> 93.1 us  [body(): pl.pallas_call(functools.partial(kernel, n, peers, bands, points, iters,...]
where the time goes in v4:
time: 97.2 us; the launch traced here: 96.5 us
  Pallas kernels  95.7 us (98%)
    pallas_call x1, Pallas kernels, body(): pl.pallas_call(functools.partial(kernel, n, peers, bands, points, iters,...  93.1 us
    pallas_call x1, Pallas kernels, body(): pl.pallas_call(functools.partial(spread, bands), out_shape=(jax.ShapeDtyp...  2.63 us

profile of v4, /device:TPU:7, one launch (start us, length us, event | category | flops | bytes accessed | tf_op | source)
XLA Modules:
  0.0 96.5 jit_solution(12003007846027820800)
XLA Ops:
  0.6 93.1 %shard_map.131 = (f32[2,2,8,40,128]{4,3,2,1,0:T(8,128)}, f32[2,2,8,32,128]{4,3,2,1,0:T(8,128)}, f32[8,128,128]{2,1,0:T(8,128)}) custom-call(f32[2,2,8,128,128]{4,3,2,1,0:T(8,128)} %coefficients.1, f32[8,128,128]{2,1,0:T(8,128)} %potential_in.1, f32[8,128,128]{2,1,0:T(8,128)} %external_in.1, f32[8,128,128]{2,1,0:T(8,128)} %core_in.1, ...), custom_call_target="tpu_custom_call" | custom-call | tf_op jit(solution)/shard_map/pallas_call | solution.py:1095
  93.7 2.6 %shard_map.132 = (f32[2,2,8,128,128]{4,3,2,1,0:T(8,128)}, f32[8,128,128]{2,1,0:T(8,128)}) custom-call(f32[2,2,8,40,128]{4,3,2,1,0:T(8,128)} %get-tuple-element.5.low, f32[2,2,8,32,128]{4,3,2,1,0:T(8,128)} %get-tuple-element.6.high, f32[8,128,128]{2,1,0:T(8,128)} %get-tuple-element.7.field), custom_call_target="tpu_custom_call" | custom-call | tf_op jit(solution)/shard_map/pallas_call | solution.py:1165

commit v5 on v4

--- a/solution.py
+++ b/solution.py
@@ -458,62 +458,59 @@
     def _():
         fixed(1).start()
 
-    def part_copy(place, target, part):
-        rows = pl.ds(0, base_rows) if part == 0 else pl.ds(base_rows, 1)
+    def part_copy(place, target, full):
+        rows = pl.ds(0, slots if full else base_rows)
         return remote(
-            sent.at[place, target, rows], got.at[place, me, rows],
-            send_sem.at[part, place], recv_sem.at[part, place], at(target),
+            sent.at[place, target, rows], got.at[place, me, rows], send_sem.at[place], recv_sem.at[place], at(target)
         )
 
-    def own_copy(place, part):
-        rows = pl.ds(0, base_rows) if part == 0 else pl.ds(base_rows, 1)
-        return pltpu.make_async_copy(sent.at[place, me, rows], got.at[place, me, rows], recv_sem.at[part, place])
+    def own_copy(place, full):
+        rows = pl.ds(0, slots if full else base_rows)
+        return pltpu.make_async_copy(sent.at[place, me, rows], got.at[place, me, rows], recv_sem.at[place])
 
     def is_extra(device):
         return jnp.logical_or(device < zone, device >= n - zone)
 
     if extra:
         assert extra == list(range(zone)) + list(range(n - zone, n))
+
+    def either(device, act):
+        if not extra:
+            act(False)
+            return
+
+        @pl.when(is_extra(device))
+        def _():
+            act(True)
+
+        @pl.when(jnp.logical_not(is_extra(device)))
+        def _():
+            act(False)
 
     def exchange(place, to_cells):
         @pl.loop(1, n)
         def _(i):
             target = lax.rem(me + i, n)
-            part_copy(place, target, 0).start()
-            if extra:
-                @pl.when(is_extra(me if to_cells else target))
-                def _():
-                    part_copy(place, target, 1).start()
-
-        own_copy(place, 0).start()
-        if extra:
-            @pl.when(is_extra(me))
-            def _():
-                own_copy(place, 1).start()
+            either(me if to_cells else target, lambda full: part_copy(place, target, full).start())
+
+        either(me, lambda full: own_copy(place, full).start())
+
+    total_rows = base_rows * n + len(extra)
+
+    def chunks(count, sem):
+        drained(level_r.at[pl.ds(0, count * planes)], sem)
 
     def received(place, to_cells):
-        drained(got.at[place, pl.ds(0, n), pl.ds(0, base_rows)], recv_sem.at[0, place])
-        if extra and to_cells:
-            drained(got.at[place, pl.ds(0, len(extra)), base_rows], recv_sem.at[1, place])
-        elif extra:
-            @pl.when(is_extra(me))
-            def _():
-                drained(got.at[place, pl.ds(0, n), base_rows], recv_sem.at[1, place])
+        if to_cells:
+            chunks(total_rows, recv_sem.at[place])
+        else:
+            either(me, lambda full: chunks(n * (base_rows + full), recv_sem.at[place]))
 
     def all_sent(place, to_cells):
-        drained(sent.at[place, pl.ds(0, n - 1), pl.ds(0, base_rows)], send_sem.at[0, place])
-        if extra and to_cells:
-            @pl.when(is_extra(me))
-            def _():
-                drained(sent.at[place, pl.ds(0, n - 1), base_rows], send_sem.at[1, place])
-        elif extra:
-            @pl.when(is_extra(me))
-            def _():
-                drained(sent.at[place, pl.ds(0, len(extra) - 1), base_rows], send_sem.at[1, place])
-
-            @pl.when(jnp.logical_not(is_extra(me)))
-            def _():
-                drained(sent.at[place, pl.ds(0, len(extra)), base_rows], send_sem.at[1, place])
+        if to_cells:
+            either(me, lambda full: chunks((n - 1) * (base_rows + full), send_sem.at[place]))
+        else:
+            either(me, lambda full: chunks(total_rows - base_rows - full, send_sem.at[place]))
 
     def outward(value_of, place):
         stacked = []
@@ -1146,8 +1143,8 @@
             dma((bands, planes)),
             dma((2, bands, slots)),
             dma((3,)),
-            dma((2, stages)),
-            dma((2, stages)),
+            dma((stages,)),
+            dma((stages,)),
             dma((2,)),
             dma((bands, slots, 2)),
             dma((bands, planes)),

time: 97.2 us -> 97.1 us (level)
  no operation moved by 1% of the time
where the time goes in v5:
time: 97.1 us; the launch traced here: 96.4 us
  Pallas kernels  95.6 us (98%)
    pallas_call x1, Pallas kernels, body(): pl.pallas_call(functools.partial(kernel, n, peers, bands, points, iters,...  92.9 us
    pallas_call x1, Pallas kernels, body(): pl.pallas_call(functools.partial(spread, bands), out_shape=(jax.ShapeDtyp...  2.63 us

profile of v5, /device:TPU:7, one launch (start us, length us, event | category | flops | bytes accessed | tf_op | source)
XLA Modules:
  0.0 96.4 jit_solution(4808704736724090985)
XLA Ops:
  0.6 92.9 %shard_map.131 = (f32[2,2,8,40,128]{4,3,2,1,0:T(8,128)}, f32[2,2,8,32,128]{4,3,2,1,0:T(8,128)}, f32[8,128,128]{2,1,0:T(8,128)}) custom-call(f32[2,2,8,128,128]{4,3,2,1,0:T(8,128)} %coefficients.1, f32[8,128,128]{2,1,0:T(8,128)} %potential_in.1, f32[8,128,128]{2,1,0:T(8,128)} %external_in.1, f32[8,128,128]{2,1,0:T(8,128)} %core_in.1, ...), custom_call_target="tpu_custom_call" | custom-call | tf_op jit(solution)/shard_map/pallas_call | solution.py:1092
  93.6 2.6 %shard_map.132 = (f32[2,2,8,128,128]{4,3,2,1,0:T(8,128)}, f32[8,128,128]{2,1,0:T(8,128)}) custom-call(f32[2,2,8,40,128]{4,3,2,1,0:T(8,128)} %get-tuple-element.5.low, f32[2,2,8,32,128]{4,3,2,1,0:T(8,128)} %get-tuple-element.6.high, f32[8,128,128]{2,1,0:T(8,128)} %get-tuple-element.7.field), custom_call_target="tpu_custom_call" | custom-call | tf_op jit(solution)/shard_map/pallas_call | solution.py:1162
